TPU v7x, 128 devices: a whole 4x4x4 slice. The times are simulated.
128 devices in a mesh: row: 4 (over y), col: 8 (over z, core), depth: 4 (over x).
Axes of the slice: x: 4, y: 4, z: 4, core: 2. Of those that a mesh axis runs over, the one named last changes fastest.
Arguments:
- panels: float32 [2, 8192, 512], P(None, ('row', 'depth'), 'col'), may hold values from -6 to 6
- slab: float32 [8192, 4096], P(('row', 'depth'), 'col'), may hold values from -6 to 6
- pivot_one: int32 [512], replicated, may hold values from 512 to 8191, as said below
- pivot_two: int32 [512], replicated, may hold values from 1024 to 8191, as said below
- lower_inv: float32 [2, 512, 512], replicated, may hold values from -1 to 1, as said below
- upper_inv: float32 [2, 512, 512], replicated, may hold values from -1 to 1, as said below
Outputs:
- panels_out: float32 [2, 8192, 512], P(None, ('row', 'depth'), 'col')
- slab_out: float32 [8192, 4096], P(('row', 'depth'), 'col')
Inputs may be any that keep to these rules, and one draw needn't show every extreme that they name: `pivot_one`: 512 distinct rows, none among the first 512. `pivot_two`: 512 distinct rows, none among the first 1024. `lower_inv`: each of the two blocks is lower triangular with ones on its diagonal. `upper_inv`: each of the two blocks is upper triangular with a positive diagonal.
All inputs are finite; a program needn't handle non-finite values.
Results may differ from a plain program's by a relative error of at most 0.000075.
Values sent between devices are 32-bit elements; how exact they have to be, the bound alone decides.
No kernel may reach another device: no remote copies, remote signals or barrier semaphores. Data moves between devices by JAX's collectives and lax.ppermute only.
A program may use at most 128 MiB of HBM per device.

v0:
```python
import jax
import jax.numpy as jnp
from jax import lax
from jax.experimental import pallas as pl
from jax.experimental.pallas import tpu as pltpu
from jax.sharding import PartitionSpec as P


NB = 512
CAP = 96
PEERS = 16
SLOTS = PEERS * CAP
HALF = (NB + 2 * CAP) // 2
RD = ("row", "depth")
F32 = jnp.float32
BF16 = jnp.bfloat16
VMEM = pl.BlockSpec(memory_space=pltpu.VMEM)
ANY = pl.BlockSpec(memory_space=pl.ANY)
SMEM = pl.BlockSpec(memory_space=pltpu.SMEM)


def iota(shape, axis):
    return lax.broadcasted_iota(jnp.int32, shape, axis)


def split2(x):
    high = x.astype(BF16)
    return high, (x - high.astype(F32)).astype(BF16)


def split3(x):
    high = x.astype(BF16)
    rest = x - high.astype(F32)
    middle = rest.astype(BF16)
    return high, middle, (rest - middle.astype(F32)).astype(BF16)


def mm(a, b):
    return jnp.dot(a, b, preferred_element_type=F32)


def dot3(a, b):
    return mm(a[0], b[0]) + (mm(a[0], b[1]) + mm(a[1], b[0]))


def pick(onehot, parts):
    return (mm(onehot, parts[0]) + mm(onehot, parts[1])) + mm(onehot, parts[2])


def pick_t(onehot, parts):
    dots = [lax.dot_general(onehot, p, (((1,), (1,)), ((), ())), preferred_element_type=F32) for p in parts]
    return (dots[0] + dots[1]) + dots[2]


def column(row):
    return jnp.transpose(jnp.broadcast_to(row, (8, row.shape[1])))[:, :1]


def running(x):
    lane = iota(x.shape, 1)
    by = 1
    while by < x.shape[1]:
        x = x + jnp.where(lane >= by, pltpu.roll(x, by, 1), 0.0)
        by *= 2
    return x


def down(mask, value):
    return jnp.sum(jnp.where(mask, value, 0.0), axis=0, keepdims=True)


def blocks_onehot(rank, code, first, count):
    k = iota((CAP, NB), 0)
    held = k == rank
    blocks = [
        jnp.where(held | ((k + (first + b) * CAP) == code), 1.0, 0.0).astype(BF16) for b in range(count)
    ]
    return jnp.concatenate(blocks, axis=0)


def plan_kernel(where_ref, one_ref, two_ref, panel_ref, at_ref, codes_ref, every_ref, most_ref, out_ref):
    me = where_ref[0]
    one, two = one_ref[...].astype(F32), two_ref[...].astype(F32)
    one_c, two_c = column(one), column(two)
    lane = iota((1, NB), 1).astype(F32)
    sub = iota((NB, 1), 0).astype(F32)
    hit = down(one_c == two, sub + 1.0)
    source = jnp.concatenate([one, jnp.where(hit > 0, hit - 1.0, two)], axis=1)
    again = down(two_c == one, 1.0) > 0
    taken = down(one_c == lane + NB, 1.0) > 0
    onward = down(sub + NB == one, two_c)
    leaves = (
        jnp.where(again, -1.0, jnp.where(one < 2 * NB, onward, one)),
        jnp.where(taken, -1.0, two),
    )
    owner = source.astype(jnp.int32) >> 9
    owners = jnp.where(iota((PEERS, 2 * NB), 0) == owner, 1.0, 0.0)
    count = running(owners)
    rank = jnp.sum(owners * count, axis=0, keepdims=True) - 1.0
    takers = [v.astype(jnp.int32) >> 9 for v in leaves]
    taker_rows = jnp.concatenate([jnp.where(iota((PEERS, NB), 0) == t, 1.0, 0.0) for t in takers], axis=0)
    taker_count = taker_rows * running(taker_rows)
    most = jnp.max(rank)
    out_codes, in_codes, out_every, in_every = [], [], [], []
    for q in range(2):
        sent = count[q:q + 1, 2 * NB - 1:]
        place = jnp.sum(taker_count[q * PEERS:(q + 1) * PEERS], axis=0, keepdims=True) - 1.0 + sent
        place = place.astype(jnp.int32)
        most = jnp.maximum(most, jnp.max(jnp.where(takers[q] < 0, 0, place).astype(F32)))
        fits = place < CAP
        out_codes.append(jnp.where((takers[q] >= 0) & fits, takers[q] * CAP + place, -1))
        in_codes.append(jnp.where(fits, place + (q * CAP + 2), 1).astype(F32))
        out_every.append(jnp.where(takers[q] >= 0, takers[q] * 4096 + place, -1))
        in_every.append((place + (q * 4096 + 1)).astype(F32))
    most_ref[0] = most.astype(jnp.int32)
    mine = lane + (me * NB).astype(F32)
    out_rank = (down(column(source) == mine, column(rank) + 1.0) - 1.0).astype(jnp.int32)
    out_code = jnp.where(me == 0, out_codes[0], jnp.where(me == 1, out_codes[1], -1))
    code = jnp.where(me == 0, out_every[0], jnp.where(me == 1, out_every[1], -1))
    hit = column(jnp.concatenate(leaves, axis=1)) == mine
    in_code = down(hit, column(jnp.concatenate(in_codes, axis=1)))
    rank = rank.astype(jnp.int32)
    at_ref[...] = jnp.where(rank < CAP, owner * CAP + rank, -1)
    codes_ref[0:1] = out_rank
    codes_ref[1:2] = out_code
    codes_ref[2:3] = in_code.astype(jnp.int32) - 2
    codes_ref[3:4] = code
    codes_ref[4:5] = code
    codes_ref[5:8] = jnp.zeros((3, NB), jnp.int32)
    every_ref[:, :2 * NB] = owner * 4096 + rank
    every_ref[:, 2 * NB:] = down(hit, column(jnp.concatenate(in_every, axis=1))).astype(jnp.int32) - 1
    parts = split3(panel_ref[...])
    for c in range(4):
        onehot = blocks_onehot(out_rank, out_code, 4 * c, 4)
        out_ref[4 * c * CAP:4 * (c + 1) * CAP] = pick_t(onehot, parts)


def make_plan(where, pivot_one, pivot_two, panel_t):
    return pl.pallas_call(
        plan_kernel,
        in_specs=[SMEM] + [VMEM] * 3,
        out_specs=[VMEM, VMEM, VMEM, SMEM, VMEM],
        out_shape=[
            jax.ShapeDtypeStruct((1, 2 * NB), jnp.int32),
            jax.ShapeDtypeStruct((8, NB), jnp.int32),
            jax.ShapeDtypeStruct((1, 3 * NB), jnp.int32),
            jax.ShapeDtypeStruct((1,), jnp.int32),
            jax.ShapeDtypeStruct((SLOTS, 128), F32),
        ],
        name="make_plan",
    )(where, pivot_one.reshape(1, NB), pivot_two.reshape(1, NB), panel_t)


def pack_kernel(codes_ref, rows_ref, out_ref, parts_ref):
    step = pl.program_id(0)

    @pl.when(step == 0)
    def _():
        for n, part in enumerate(split3(rows_ref[...])):
            parts_ref[n] = part

    onehot = blocks_onehot(codes_ref[0:1], codes_ref[1:2], step * 4, 4)
    out_ref[...] = pick(onehot, (parts_ref[0], parts_ref[1], parts_ref[2]))


def pack(codes, rows):
    width = rows.shape[1]
    return pl.pallas_call(
        pack_kernel,
        grid=(4,),
        in_specs=[pl.BlockSpec((8, NB), lambda i: (0, 0)), pl.BlockSpec((NB, width), lambda i: (0, 0))],
        out_specs=pl.BlockSpec((4 * CAP, width), lambda i: (i, 0)),
        out_shape=jax.ShapeDtypeStruct((SLOTS, width), F32),
        scratch_shapes=[pltpu.VMEM((3, NB, width), BF16)],
        name="pack_rows",
    )(codes, rows)


def slots_of(at_ref, n):
    at = column(at_ref[:, n * NB:(n + 1) * NB])
    return jnp.where(iota((NB, SLOTS), 1) == at, 1.0, 0.0).astype(BF16)


def arrivals(codes_ref):
    code = column(codes_ref[2:3])
    return jnp.where(iota((NB, 2 * CAP), 1) == code, 1.0, 0.0).astype(BF16), code > -2


def late(flag_ref, extra_ref, buffer, sem):
    @pl.when(flag_ref[0] < CAP)
    def _():
        buffer[...] = jnp.zeros_like(buffer)

    @pl.when(flag_ref[0] >= CAP)
    def _():
        copy = pltpu.make_async_copy(extra_ref, buffer, sem)
        copy.start()
        copy.wait()

    return buffer


def panel_rows_kernel(where_ref, flag_ref, at_ref, got_ref, extra_ref, keep_ref, send_ref, tops_ref, more, sem):
    core = where_ref[1]
    more = late(flag_ref, extra_ref.at[:2 * NB, :128], more, sem)
    parts = split3(got_ref[...])
    first = pick(slots_of(at_ref, 0), parts) + more[:NB]
    second = pick(slots_of(at_ref, 1), parts) + more[NB:]
    left = iota((NB, 128), 1) < 64
    tops_ref[...] = jnp.where(left, first, second)
    swapped = jnp.where(left, second, first)
    upper = swapped[:HALF]
    lower = jnp.concatenate([swapped[HALF:], got_ref[:2 * CAP]], axis=0)
    keep_ref[...] = jnp.where(core == 0, upper, lower)
    send_ref[...] = jnp.where(core == 0, lower, upper)


def panel_rows(where, flag, at, got, extra):
    half = jax.ShapeDtypeStruct((HALF, 128), F32)
    return pl.pallas_call(
        panel_rows_kernel,
        in_specs=[SMEM] * 2 + [VMEM] * 2 + [ANY],
        out_specs=[VMEM] * 3,
        out_shape=[half, half, jax.ShapeDtypeStruct((NB, 128), F32)],
        scratch_shapes=[pltpu.VMEM((2 * NB, 128), F32), pltpu.SemaphoreType.DMA],
        name="panel_rows",
    )(where, flag, at, got, extra)


def fold_kernel(at_ref, lower_ref, one_ref, two_ref):
    for n, out in enumerate((one_ref, two_ref)):
        onehot = slots_of(at_ref, n)
        high, low = split2(lower_ref[n])
        out[0] = mm(high, onehot).astype(BF16)
        out[1] = mm(low, onehot).astype(BF16)


def fold(at, lower_inv):
    shape = jax.ShapeDtypeStruct((2, NB, SLOTS), BF16)
    return pl.pallas_call(
        fold_kernel, in_specs=[VMEM] * 2, out_specs=[VMEM] * 2, out_shape=[shape, shape], name="fold_slots"
    )(at, lower_inv)


def own_panels_kernel(where_ref, *refs):
    pieces, out_ref, gath = refs[:8], refs[8], refs[9]
    col = where_ref[3]
    for m in range(8):
        gath[lax.bitwise_xor(col, m)] = pieces[m][...]
    for n in range(2):
        whole = jnp.concatenate([gath[c, 64 * n:64 * (n + 1)] for c in range(8)], axis=0)
        out_ref[n] = jnp.transpose(whole)


def own_panels(where, pieces):
    return pl.pallas_call(
        own_panels_kernel,
        in_specs=[SMEM] + [VMEM] * 8,
        out_specs=VMEM,
        out_shape=jax.ShapeDtypeStruct((2, NB, NB), F32),
        scratch_shapes=[pltpu.VMEM((8, 128, NB), F32)],
        name="own_panels",
    )(where, *pieces)


def panel_math_kernel(where_ref, flag_ref, codes_ref, tops_ref, whole_ref, extra_ref, k0, k1, k2, k3, p0, p1, p2, p3,
                      lower_ref, upper_ref, left_ref, pout_ref, gath, src, more, sem):
    me, core, z = where_ref[0], where_ref[1], where_ref[2]
    for s, (a, b) in enumerate(((k0, p0), (k1, p1), (k2, p2), (k3, p3))):
        zz = lax.rem(z + 4 - s, 4)
        gath[core, zz] = a[...]
        gath[1 - core, zz] = b[...]
    more = late(flag_ref, extra_ref, more, sem)
    left = iota((2 * HALF, 128), 1) < 64
    ones, twos = [], []
    for zz in range(4):
        a = jnp.concatenate([gath[0, zz, :HALF], gath[1, zz, HALF:]], axis=0)
        b = jnp.concatenate([gath[0, zz, HALF:], gath[1, zz, :HALF]], axis=0)
        ones.append(jnp.where(left, a, pltpu.roll(b, 64, 1)))
        twos.append(jnp.where(left, pltpu.roll(a, 64, 1), b))
    in_one, in_two = jnp.concatenate(ones, axis=1), jnp.concatenate(twos, axis=1)
    onehot, moved = arrivals(codes_ref)
    top_two_one, top_one_two = in_one[:NB], in_two[:NB]
    own_one = jnp.where(moved, pick(onehot, split3(in_one[NB:])) + more[0], whole_ref[0])
    own_two = jnp.where(moved, pick(onehot, split3(in_two[NB:])) + more[1], whole_ref[1])
    own_one = jnp.where(me == 1, top_two_one, own_one)
    own_two = jnp.where(me == 1, 0.0, own_two)
    upper_one_inv = split2(upper_ref[0])
    lower_kept = dot3(split2(own_one), upper_one_inv)
    lower_top = dot3(split2(top_two_one), upper_one_inv)
    upper_panel = dot3(split2(lower_ref[0]), split2(top_one_two))
    kept_parts = split2(lower_kept)
    updated = own_two - dot3(kept_parts, split2(upper_panel))
    lower_two = dot3(split2(updated), split2(upper_ref[1]))
    left_ref[0], left_ref[1] = kept_parts
    left_ref[2], left_ref[3] = split2(lower_two)
    left_ref[4], left_ref[5] = split2(dot3(split2(lower_ref[1]), split2(lower_top)))
    src[0] = lower_kept
    src[1] = jnp.where(me == 0, upper_panel, jnp.where(me == 1, updated, lower_two))
    at = pl.multiple_of(z * 128, 128)
    one = src[0, :, pl.ds(at, 128)]
    two = src[1, :, pl.ds(at, 128)]
    left = iota((NB, 128), 1) < 64
    mine = jnp.where(
        core == 0,
        jnp.where(left, one, pltpu.roll(two, 64, 1)),
        jnp.where(left, pltpu.roll(one, 64, 1), two),
    )
    tops = tops_ref[...]
    mine = jnp.where(left & (me == 0), tops, mine)
    mine = jnp.where(jnp.logical_not(left) & (me == 1), tops + mine, mine)
    pout_ref[...] = jnp.transpose(mine)


def panel_math(where, flag, codes, tops, whole, extra, kept, other, lower_inv, upper_inv):
    return pl.pallas_call(
        panel_math_kernel,
        in_specs=[SMEM] * 2 + [VMEM] * 3 + [ANY] + [VMEM] * 10,
        out_specs=[VMEM] * 2,
        out_shape=[jax.ShapeDtypeStruct((6, NB, NB), BF16), jax.ShapeDtypeStruct((128, NB), F32)],
        scratch_shapes=[
            pltpu.VMEM((2, 4, 2 * HALF, 128), F32),
            pltpu.VMEM((2, NB, NB), F32),
            pltpu.VMEM((2, NB, NB), F32),
            pltpu.SemaphoreType.DMA,
        ],
        name="panel_math",
    )(where, flag, codes, tops, whole, extra, *kept, *other, lower_inv, upper_inv)


WIDE = 256


def slab_kernel(where_ref, flag_ref, codes_ref, got_ref, rows_ref, extra_ref, one_ref, two_ref, left_ref, out_ref,
                more, sem):
    me = where_ref[0]
    at = pl.multiple_of(pl.program_id(0) * WIDE, WIDE)
    more = late(flag_ref, extra_ref.at[:, pl.ds(at, WIDE)], more, sem)
    got = split2(got_ref[...])
    upper_one = dot3((one_ref[0], one_ref[1]), got) + more[:NB]
    one = split2(upper_one)
    upper_two = (dot3((two_ref[0], two_ref[1]), got) - dot3((left_ref[4], left_ref[5]), one)) + more[NB:2 * NB]

    @pl.when(me == 0)
    def _():
        out_ref[...] = upper_one

    @pl.when(me == 1)
    def _():
        out_ref[...] = upper_two

    @pl.when(me > 1)
    def _():
        onehot, moved = arrivals(codes_ref)
        own = jnp.where(moved, pick(onehot, split3(got_ref[:2 * CAP])) + more[2 * NB:], rows_ref[...])
        two = split2(upper_two)
        out_ref[...] = own - dot3((left_ref[0], left_ref[1]), one) - dot3((left_ref[2], left_ref[3]), two)


def slab_math(where, flag, codes, got, rows, extra, one, two, left):
    whole = lambda *shape: pl.BlockSpec(shape, lambda i: (0,) * len(shape))
    return pl.pallas_call(
        slab_kernel,
        grid=(NB // WIDE,),
        in_specs=[
            SMEM,
            SMEM,
            whole(8, NB),
            pl.BlockSpec((SLOTS, WIDE), lambda i: (0, i)),
            pl.BlockSpec((NB, WIDE), lambda i: (0, i)),
            ANY,
            whole(2, NB, SLOTS),
            whole(2, NB, SLOTS),
            whole(6, NB, NB),
        ],
        out_specs=pl.BlockSpec((NB, WIDE), lambda i: (0, i)),
        out_shape=jax.ShapeDtypeStruct((NB, NB), F32),
        scratch_shapes=[pltpu.VMEM((3 * NB, WIDE), F32), pltpu.SemaphoreType.DMA],
        name="slab_math",
    )(where, flag, codes, got, rows, extra, one, two, left)


def mark_kernel(in_ref, out_ref):
    out_ref[0] = in_ref[0]


def mark(x):
    return pl.pallas_call(
        mark_kernel, in_specs=[SMEM], out_specs=SMEM, out_shape=jax.ShapeDtypeStruct((1,), jnp.int32), name="mark"
    )(x)


def exchange(blocks):
    width = blocks.shape[1]
    return lax.all_to_all(blocks.reshape(PEERS, CAP, width), RD, 0, 0).reshape(SLOTS, width)


def unused_kernel(*refs):
    pass


def unwritten(*shapes):
    return pl.pallas_call(
        unused_kernel,
        out_specs=[ANY] * len(shapes),
        out_shape=[jax.ShapeDtypeStruct(shape, F32) for shape in shapes],
        name="unwritten",
    )()


def late_pack_kernel(base_ref, codes_ref, panel_ref, rows_ref, out_ref):
    k = iota((CAP, NB), 0) + base_ref[0]
    picked = (k == codes_ref[0:1]) | ((k + pl.program_id(0) * 4096) == codes_ref[4:5])
    onehot = jnp.where(picked, 1.0, 0.0).astype(BF16)
    out_ref[:, :128] = pick_t(onehot, split3(panel_ref[...]))
    out_ref[:, 128:] = pick(onehot, split3(rows_ref[...]))


def late_pack(base, codes, panel_t, slab):
    whole = lambda *shape: pl.BlockSpec(shape, lambda i: (0,) * len(shape))
    return pl.pallas_call(
        late_pack_kernel,
        grid=(PEERS,),
        in_specs=[SMEM, whole(8, NB), whole(128, NB), whole(NB, NB)],
        out_specs=pl.BlockSpec((CAP, 128 + NB), lambda i: (i, 0)),
        out_shape=jax.ShapeDtypeStruct((SLOTS, 128 + NB), F32),
        name="late_pack",
    )(base, codes, panel_t, slab)


def late_place_kernel(base_ref, every_ref, got_ref, old_ref, out_ref):
    code = column(every_ref[...])
    place = (code & 4095) - base_ref[0]
    now = (code >= 0) & (place >= 0) & (place < CAP)
    at = jnp.where(now, (code >> 12) * CAP + place, -1)
    onehot = jnp.where(iota((128, SLOTS), 1) == at, 1.0, 0.0).astype(BF16)
    old = jnp.where(base_ref[0] == CAP, 0.0, old_ref[...])
    out_ref[...] = jnp.where(now, pick(onehot, split3(got_ref[...])), old)


def late_place(base, every, got, old):
    block = pl.BlockSpec((128, 128 + NB), lambda i: (i, 0))
    return pl.pallas_call(
        late_place_kernel,
        grid=(12,),
        in_specs=[
            SMEM,
            pl.BlockSpec((1, 128), lambda i: (0, i)),
            pl.BlockSpec((SLOTS, 128 + NB), lambda i: (0, 0)),
            block,
        ],
        out_specs=block,
        out_shape=jax.ShapeDtypeStruct((3 * NB, 128 + NB), F32),
        name="late_place",
    )(base, every, got, old)


def late_product_kernel(lower_ref, rows_ref, out_ref):
    n = pl.program_id(0)

    @pl.when(n < 8)
    def _():
        out_ref[...] = dot3(split2(lower_ref[0]), split2(rows_ref[:, 128:]))

    @pl.when(n >= 8)
    def _():
        at = pl.multiple_of(lax.rem(n, 4) * 128, 128)
        out_ref[...] = rows_ref[pl.ds(at, 128), 128:]


def late_product(lower_inv, rows):
    return pl.pallas_call(
        late_product_kernel,
        grid=(12,),
        in_specs=[
            pl.BlockSpec((1, 128, NB), lambda i: (lax.min(i // 4, 1), i % 4, 0)),
            pl.BlockSpec((NB, 128 + NB), lambda i: (i // 4, 0)),
        ],
        out_specs=pl.BlockSpec((128, NB), lambda i: (i, 0)),
        out_shape=jax.ShapeDtypeStruct((3 * NB, NB), F32),
        name="late_product",
    )(lower_inv, rows)


def late_panel_kernel(in_ref, out_ref):
    left = iota((NB, 128), 1) < 64
    a, b = in_ref[0], in_ref[1]
    out_ref[0] = jnp.where(left, a, pltpu.roll(b, 64, 1))
    out_ref[1] = jnp.where(left, pltpu.roll(a, 64, 1), b)


def late_panel(pieces):
    return pl.pallas_call(
        late_panel_kernel,
        grid=(4,),
        in_specs=[pl.BlockSpec((2, NB, 128), lambda i: (i, 0, 0))],
        out_specs=pl.BlockSpec((2, NB, 128), lambda i: (0, 0, i)),
        out_shape=jax.ShapeDtypeStruct((2, NB, NB), F32),
        name="late_panel",
    )(pieces)


def late_exchange(blocks, me):
    ring = [(i, (i + 1) % PEERS) for i in range(PEERS)]

    def turn(t, state):
        held, got = state
        mine = lax.dynamic_slice_in_dim(held, me * CAP, CAP, 0)
        got = lax.dynamic_update_slice_in_dim(got, mine, (me - t) % PEERS * CAP, 0)
        return lax.ppermute(held, RD, ring), got

    return lax.fori_loop(0, PEERS, turn, (blocks, jnp.zeros(blocks.shape, F32)))[1]


def late_gather(rows, col):
    ring = [(i, (i + 1) % 8) for i in range(8)]

    def turn(t, state):
        held, got = state
        got = lax.dynamic_update_slice_in_dim(got, held[None], (col - t) % 8, 0)
        return lax.ppermute(held, "col", ring), got

    return lax.fori_loop(0, 8, turn, (rows, jnp.zeros((8, *rows.shape), F32)))[1]


def further_rounds(most, codes, every, panel_t, slab, lower_inv, me, col):
    def turn(state):
        r, rows = state[:2]
        base = (r * CAP).reshape(1)
        got = late_exchange(late_pack(base, codes, panel_t, slab), me)
        rows = late_place(base, every, got, rows)
        wide = late_panel(late_gather(rows[2 * NB:, :128], col))
        return r + 1, rows, wide, late_product(lower_inv, rows)

    start = (jnp.int32(1), *unwritten((3 * NB, 128 + NB), (2, NB, NB), (3 * NB, NB)))
    return lax.while_loop(lambda s: s[0] * CAP <= most, turn, start)[1:]


def partner(x, by=1):
    return lax.ppermute(x, "col", [(c, c ^ by) for c in range(8)])


def shift(x, by):
    return lax.ppermute(x, "col", [(c, (c // 2 + by) % 4 * 2 + c % 2) for c in range(8)])


def body(panels, slab, pivot_one, pivot_two, lower_inv, upper_inv):
    me = lax.axis_index(RD)
    col = lax.axis_index("col")
    where = jnp.stack([me, col % 2, col // 2, col]).astype(jnp.int32)
    panel_t = jnp.swapaxes(panels, 1, 2).reshape(128, NB)
    at, codes, every, most, blocks = make_plan(where, pivot_one, pivot_two, panel_t)
    got_panel = exchange(blocks)
    pieces = [panel_t] + [partner(panel_t, by) for by in range(1, 8)]
    whole = own_panels(where, pieces)
    blocks = pack(codes, slab)
    most = mark(most)
    late_rows, late_own, late_slab = further_rounds(most[0], codes, every, panel_t, slab, lower_inv, me, col)
    got_slab = exchange(blocks)
    keep, send, tops = panel_rows(where, most, at, got_panel, late_rows)
    pair = jnp.concatenate([keep, partner(send)], axis=0)
    shifted = [shift(pair, by) for by in (1, 2, 3)]
    one, two = fold(at, lower_inv)
    shifted, one, two = lax.optimization_barrier((shifted, one, two))
    kept = [pair] + shifted
    other = [partner(x) for x in kept]
    left, panel_out = panel_math(where, most, codes, tops, whole, late_own, kept, other, lower_inv, upper_inv)
    slab_out = slab_math(where, most, codes, got_slab, slab, late_slab, one, two, left)
    return jnp.swapaxes(panel_out.reshape(2, 64, NB), 1, 2), slab_out


def solution(mesh):
    placed = (P(None, RD, "col"), P(RD, "col"), P(), P(), P(), P())
    return jax.shard_map(
        body,
        mesh=mesh,
        in_specs=placed,
        out_specs=(P(None, RD, "col"), P(RD, "col")),
        check_vma=False,
    )
```

profile of v0, /device:TPU:5, one launch (start us, length us, event | category | flops | bytes accessed | tf_op | source)
XLA Modules:
  0.0 129.0 jit_solution(1296886588989149710)
XLA Ops:
  0.7 0.6 pad_add_fusion.where_ref
  1.2 6.1 %make_plan.1 = (s32[1,1024]{1,0:T(1,128)}, s32[8,512]{1,0:T(8,128)S(1)}, s32[1,1536]{1,0:T(1,128)S(1)}, s32[1]{0:T(128)}, f32[1536,128]{1,0:T(8,128)}) custom-call(s32[4]{0:T(128)} %pad_add_fusion.where_ref, s32[1,512]{1,0:T(1,128)} %bitcast.29, s32[1,512]{1,0:T(1,128)} %bitcast.30, f32[128,512]{1,0:T(8,128)} %bitcast.24), custom_call_target="tpu_custom_call" | custom-call | tf_op jit(solution)/shard_map/make_plan/pallas_call | solution.py:139
  7.3 6.9 %all-to-all-start = ((f32[16,96,128]{2,1,0:T(8,128)}), f32[16,96,128]{2,1,0:T(8,128)S(1)}, u32[]{:S(2)}, u32[]{:S(2)}) async-start(f32[16,96,128]{2,1,0:T(8,128)} %bitcast.28), calls=%async_computation | async-start | bytes 1572864 | tf_op jit(solution)/shard_map/all_to_all | solution.py:395
  14.2 1.1 mark.1.flag_ref
  15.3 5.7 %pack_rows.1 = f32[1536,512]{1,0:T(8,128)} custom-call(s32[8,512]{1,0:T(8,128)S(1)} %get-tuple-element.810.codes_ref, f32[512,512]{1,0:T(8,128)} %rows_ref.3), custom_call_target="tpu_custom_call" | custom-call | tf_op jit(solution)/shard_map/pack_rows/pallas_call | solution.py:168
  20.9 5.5 %all-to-all-done = f32[16,96,128]{2,1,0:T(8,128)S(1)} async-done(((f32[16,96,128]{2,1,0:T(8,128)}), f32[16,96,128]{2,1,0:T(8,128)S(1)}, u32[]{:S(2)}, u32[]{:S(2)}) %all-to-all-start) | async-done | bytes 786464 | tf_op jit(solution)/shard_map/all_to_all | solution.py:395
  26.4 0.9 copy-done.5
  27.3 5.5 %all-to-all-start.1 = ((f32[16,96,512]{2,1,0:T(8,128)}), f32[16,96,512]{2,1,0:T(8,128)}, u32[]{:S(2)}, u32[]{:S(2)}) async-start(f32[16,96,512]{2,1,0:T(8,128)} %bitcast.26), calls=%async_computation.1 | async-start | bytes 6291456 | tf_op jit(solution)/shard_map/all_to_all | solution.py:395
  32.8 0.6 while.66
  33.4 0.0 copy-start
  33.4 5.9 %panel_rows.1 = (f32[352,128]{1,0:T(8,128)}, f32[352,128]{1,0:T(8,128)}, f32[512,128]{1,0:T(8,128)}) custom-call(s32[4]{0:T(128)} %pad_add_fusion.where_ref, s32[1]{0:T(128)} %mark.1.flag_ref, s32[1,1024]{1,0:T(1,128)} %get-tuple-element.528.at_ref, f32[1536,128]{1,0:T(8,128)} %bitcast.27, f32[1536,640]{1,0:T(8,128)} %get-tuple-element.890), custom_call_target="tpu_custom_call" | custom-call | tf_op jit(solution)/shard_map/panel_rows/pallas_call | solution.py:220
  39.3 2.8 %collective-permute-start.9 = (f32[352,128]{1,0:T(8,128)}, f32[352,128]{1,0:T(8,128)S(1)}, u32[]{:S(2)}, u32[]{:S(2)}) collective-permute-start(f32[352,128]{1,0:T(8,128)} %get-tuple-element.538), channel_id=1, source_target_pairs={{0,4},{4,0},{8,12},{12,8},{16,20},{20,16},{24,28},{28,24},{1,5},{5... | collective-permute-start | bytes 540680 | tf_op jit(solution)/shard_map/ppermute | solution.py:540
  42.1 0.9 constant_dynamic-update-slice_fusion.1
  43.0 0.3 collective-permute-done.9
  43.4 0.0 copy-start.6
  43.4 1.7 %collective-permute-start.10 = (f32[704,128]{1,0:T(8,128)S(1)}, f32[704,128]{1,0:T(8,128)S(1)}, u32[]{:S(2)}, u32[]{:S(2)}) collective-permute-start(f32[704,128]{1,0:T(8,128)S(1)} %constant_dynamic-update-slice_fusion.k0), channel_id=1, source_target_pairs={{0,8},{4,12},{8,16},{12,20},{16,24},{20,28},{24,0},{28,4},{1,9},{5... | collective-permute-start | bytes 1081352 | tf_op jit(solution)/shard_map/ppermute | solution.py:544
  45.1 3.3 %collective-permute-start.11 = (f32[704,128]{1,0:T(8,128)S(1)}, f32[704,128]{1,0:T(8,128)S(1)}, u32[]{:S(2)}, u32[]{:S(2)}) collective-permute-start(f32[704,128]{1,0:T(8,128)S(1)} %constant_dynamic-update-slice_fusion.k0), channel_id=1, source_target_pairs={{0,16},{4,20},{8,24},{12,28},{16,0},{20,4},{24,8},{28,12},{1,17},{... | collective-permute-start | bytes 1081352 | tf_op jit(solution)/shard_map/ppermute | solution.py:544
  48.4 0.9 collective-permute-start.2
  49.3 0.7 collective-permute-start.12
  50.0 0.7 collective-permute-start.3
  50.8 0.0 collective-permute-done.2.refs_1_
  50.8 1.2 collective-permute-start.4
  52.0 3.8 %collective-permute-done.10.k1 = f32[704,128]{1,0:T(8,128)S(1)} collective-permute-done((f32[704,128]{1,0:T(8,128)S(1)}, f32[704,128]{1,0:T(8,128)S(1)}, u32[]{:S(2)}, u32[]{:S(2)}) %collective-permute-start.10) | collective-permute-done | bytes 360480 | tf_op jit(solution)/shard_map/ppermute | solution.py:544
  55.7 1.5 %collective-permute-start.5 = (f32[128,512]{1,0:T(8,128)S(1)}, f32[128,512]{1,0:T(8,128)}, u32[]{:S(2)}, u32[]{:S(2)}) collective-permute-start(f32[128,512]{1,0:T(8,128)S(1)} %get-tuple-element.895), channel_id=1, source_target_pairs={{0,16},{4,20},{8,24},{12,28},{16,0},{20,4},{24,8},{28,12},{1,17},{... | collective-permute-start | bytes 786440 | tf_op jit(solution)/shard_map/ppermute | solution.py:540
  57.2 7.2 %collective-permute-done.11.k2 = f32[704,128]{1,0:T(8,128)S(1)} collective-permute-done((f32[704,128]{1,0:T(8,128)S(1)}, f32[704,128]{1,0:T(8,128)S(1)}, u32[]{:S(2)}, u32[]{:S(2)}) %collective-permute-start.11) | collective-permute-done | bytes 360480 | tf_op jit(solution)/shard_map/ppermute | solution.py:544
  64.4 1.5 %collective-permute-start.6 = (f32[128,512]{1,0:T(8,128)S(1)}, f32[128,512]{1,0:T(8,128)}, u32[]{:S(2)}, u32[]{:S(2)}) collective-permute-start(f32[128,512]{1,0:T(8,128)S(1)} %get-tuple-element.895), channel_id=1, source_target_pairs={{0,20},{4,16},{8,28},{12,24},{16,4},{20,0},{24,12},{28,8},{1,21},{... | collective-permute-start | bytes 786440 | tf_op jit(solution)/shard_map/ppermute | solution.py:540
  65.9 0.0 collective-permute-done.12.k3
  65.9 0.7 copy-done.9
  66.7 1.1 collective-permute-start.7
  67.8 6.7 %fold_slots.1 = (bf16[2,512,1536]{2,1,0:T(8,128)(2,1)}, bf16[2,512,1536]{2,1,0:T(8,128)(2,1)}) custom-call(s32[1,1024]{1,0:T(1,128)} %get-tuple-element.528.at_ref, f32[2,512,512]{2,1,0:T(8,128)S(1)} %copy-done), custom_call_target="tpu_custom_call" | custom-call | tf_op jit(solution)/shard_map/fold_slots/pallas_call | solution.py:240
  74.5 0.0 collective-permute-done.3.refs_2_
  74.5 0.6 collective-permute-start.13
  75.1 1.6 %collective-permute-done.4.refs_3_ = f32[128,512]{1,0:T(8,128)} collective-permute-done((f32[128,512]{1,0:T(8,128)S(1)}, f32[128,512]{1,0:T(8,128)}, u32[]{:S(2)}, u32[]{:S(2)}) %collective-permute-start.4) | collective-permute-done | bytes 262176 | tf_op jit(solution)/shard_map/ppermute | solution.py:540
  76.8 0.0 collective-permute-start.14
  76.8 4.4 %collective-permute-done.5.refs_4_ = f32[128,512]{1,0:T(8,128)} collective-permute-done((f32[128,512]{1,0:T(8,128)S(1)}, f32[128,512]{1,0:T(8,128)}, u32[]{:S(2)}, u32[]{:S(2)}) %collective-permute-start.5) | collective-permute-done | bytes 262176 | tf_op jit(solution)/shard_map/ppermute | solution.py:540
  81.2 2.1 %collective-permute-start.15 = (f32[704,128]{1,0:T(8,128)}, f32[704,128]{1,0:T(8,128)}, u32[]{:S(2)}, u32[]{:S(2)}) collective-permute-start(f32[704,128]{1,0:T(8,128)} %copy-done.8), channel_id=1, source_target_pairs={{0,4},{4,0},{8,12},{12,8},{16,20},{20,16},{24,28},{28,24},{1,5},{5... | collective-permute-start | bytes 1081352 | tf_op jit(solution)/shard_map/ppermute | solution.py:540
  83.3 4.1 %collective-permute-done.6.refs_5_ = f32[128,512]{1,0:T(8,128)} collective-permute-done((f32[128,512]{1,0:T(8,128)S(1)}, f32[128,512]{1,0:T(8,128)}, u32[]{:S(2)}, u32[]{:S(2)}) %collective-permute-start.6) | collective-permute-done | bytes 262176 | tf_op jit(solution)/shard_map/ppermute | solution.py:540
  87.4 0.0 collective-permute-start.16
  87.4 0.0 collective-permute-done.7.refs_6_
  87.4 2.3 %collective-permute-start.8 = (f32[128,512]{1,0:T(8,128)S(1)}, f32[128,512]{1,0:T(8,128)}, u32[]{:S(2)}, u32[]{:S(2)}) collective-permute-start(f32[128,512]{1,0:T(8,128)S(1)} %get-tuple-element.895), channel_id=1, source_target_pairs={{0,28},{4,24},{8,20},{12,16},{16,12},{20,8},{24,4},{28,0},{1,29},{... | collective-permute-start | bytes 786440 | tf_op jit(solution)/shard_map/ppermute | solution.py:540
  89.7 7.5 %collective-permute-done.8.refs_7_ = f32[128,512]{1,0:T(8,128)} collective-permute-done((f32[128,512]{1,0:T(8,128)S(1)}, f32[128,512]{1,0:T(8,128)}, u32[]{:S(2)}, u32[]{:S(2)}) %collective-permute-start.8) | collective-permute-done | bytes 262176 | tf_op jit(solution)/shard_map/ppermute | solution.py:540
  97.2 3.5 %own_panels.1.whole_ref = f32[2,512,512]{2,1,0:T(8,128)} custom-call(s32[4]{0:T(128)} %pad_add_fusion.where_ref, f32[128,512]{1,0:T(8,128)S(1)} %get-tuple-element.895, f32[128,512]{1,0:T(8,128)} %copy-done.10, f32[128,512]{1,0:T(8,128)} %collective-permute-done.3.refs_2_, f32[128,512]{1,0:T(8,128)} %collective-permute-done.4.refs_3_, ...), custom_call_target="tpu_custom_call" | custom-call | tf_op jit(solution)/shard_map/own_panels/pallas_call | solution.py:256
  100.7 0.0 collective-permute-done.13.p0
  100.7 0.0 collective-permute-done.14.p1
  100.7 0.0 collective-permute-done.16.p3
  100.7 0.0 copy-start.3
  100.8 13.0 %panel_math.1 = (bf16[6,512,512]{2,1,0:T(8,128)(2,1)}, f32[128,512]{1,0:T(8,128)}) custom-call(s32[4]{0:T(128)} %pad_add_fusion.where_ref, s32[1]{0:T(128)} %mark.1.flag_ref, s32[8,512]{1,0:T(8,128)S(1)} %get-tuple-element.894, f32[512,128]{1,0:T(8,128)} %get-tuple-element.535.tops_ref, f32[2,512,512]{2,1,0:T(8,128)} %own_panels.1.whole_ref, ...), custom_call_target="tpu_custom_call" | custom-call | tf_op jit(solution)/shard_map/panel_math/pallas_call | solution.py:316
  113.8 15.0 %slab_math.1 = f32[512,512]{1,0:T(8,128)} custom-call(s32[4]{0:T(128)} %pad_add_fusion.where_ref, s32[1]{0:T(128)} %mark.1.flag_ref, s32[8,512]{1,0:T(8,128)S(1)} %get-tuple-element.894, f32[1536,512]{1,0:T(8,128)} %bitcast.17.got_ref, f32[512,512]{1,0:T(8,128)S(1)} %copy-done.3, f32[1536,512]{1,0:T(8,128)} %get-tuple-element.892, ...), custom_call_target="tpu_custom_call" | custom-call | tf_op jit(solution)/shard_map/slab_math/pallas_call | solution.py:362
  (19 shorter events, 0.0 us)
Async XLA Ops:
  7.3 19.1 %all-to-all-start = ((f32[16,96,128]{2,1,0:T(8,128)}), f32[16,96,128]{2,1,0:T(8,128)S(1)}, u32[]{:S(2)}, u32[]{:S(2)}) async-start(f32[16,96,128]{2,1,0:T(8,128)} %bitcast.28), calls=%async_computation | async-start | bytes 1572864 | tf_op jit(solution)/shard_map/all_to_all | solution.py:395
  26.4 0.9 copy-start.5
  27.3 5.5 %copy-start.1 = (f32[512,512]{1,0:T(8,128)S(1)}, f32[512,512]{1,0:T(8,128)}, u32[]{:S(2)}) copy-start(f32[512,512]{1,0:T(8,128)} %rows_ref.3) | copy-start | bytes 3145732
  27.3 5.5 %copy-start.4 = (f32[2,512,64]{1,2,0:T(8,128)S(1)}, f32[2,512,64]{1,2,0:T(8,128)}, u32[]{:S(2)}) copy-start(f32[2,512,64]{1,2,0:T(8,128)} %param.12) | copy-start | bytes 786436
  27.3 86.5 %all-to-all-start.1 = ((f32[16,96,512]{2,1,0:T(8,128)}), f32[16,96,512]{2,1,0:T(8,128)}, u32[]{:S(2)}, u32[]{:S(2)}) async-start(f32[16,96,512]{2,1,0:T(8,128)} %bitcast.26), calls=%async_computation.1 | async-start | bytes 6291456 | tf_op jit(solution)/shard_map/all_to_all | solution.py:395
  33.4 34.4 %copy-start = (f32[2,512,512]{2,1,0:T(8,128)S(1)}, f32[2,512,512]{2,1,0:T(8,128)}, u32[]{:S(2)}) copy-start(f32[2,512,512]{2,1,0:T(8,128)} %get-tuple-element.901) | copy-start | bytes 6291460
  39.3 4.0 %collective-permute-start.9 = (f32[352,128]{1,0:T(8,128)}, f32[352,128]{1,0:T(8,128)S(1)}, u32[]{:S(2)}, u32[]{:S(2)}) collective-permute-start(f32[352,128]{1,0:T(8,128)} %get-tuple-element.538), channel_id=1, source_target_pairs={{0,4},{4,0},{8,12},{12,8},{16,20},{20,16},{24,28},{28,24},{1,5},{5... | collective-permute-start | bytes 540680 | tf_op jit(solution)/shard_map/ppermute | solution.py:540
  43.4 57.3 %copy-start.6 = (f32[704,128]{1,0:T(8,128)}, f32[704,128]{1,0:T(8,128)S(1)}, u32[]{:S(2)}) copy-start(f32[704,128]{1,0:T(8,128)S(1)} %constant_dynamic-update-slice_fusion.k0) | copy-start | bytes 1081348
  43.4 12.4 %collective-permute-start.10 = (f32[704,128]{1,0:T(8,128)S(1)}, f32[704,128]{1,0:T(8,128)S(1)}, u32[]{:S(2)}, u32[]{:S(2)}) collective-permute-start(f32[704,128]{1,0:T(8,128)S(1)} %constant_dynamic-update-slice_fusion.k0), channel_id=1, source_target_pairs={{0,8},{4,12},{8,16},{12,20},{16,24},{20,28},{24,0},{28,4},{1,9},{5... | collective-permute-start | bytes 1081352 | tf_op jit(solution)/shard_map/ppermute | solution.py:544
  45.1 19.3 %collective-permute-start.11 = (f32[704,128]{1,0:T(8,128)S(1)}, f32[704,128]{1,0:T(8,128)S(1)}, u32[]{:S(2)}, u32[]{:S(2)}) collective-permute-start(f32[704,128]{1,0:T(8,128)S(1)} %constant_dynamic-update-slice_fusion.k0), channel_id=1, source_target_pairs={{0,16},{4,20},{8,24},{12,28},{16,0},{20,4},{24,8},{28,12},{1,17},{... | collective-permute-start | bytes 1081352 | tf_op jit(solution)/shard_map/ppermute | solution.py:544
  48.4 2.4 %collective-permute-start.2 = (f32[128,512]{1,0:T(8,128)S(1)}, f32[128,512]{1,0:T(8,128)S(1)}, u32[]{:S(2)}, u32[]{:S(2)}) collective-permute-start(f32[128,512]{1,0:T(8,128)S(1)} %get-tuple-element.895), channel_id=1, source_target_pairs={{0,4},{4,0},{8,12},{12,8},{16,20},{20,16},{24,28},{28,24},{1,5},{5... | collective-permute-start | bytes 786440 | tf_op jit(solution)/shard_map/ppermute | solution.py:540
  49.3 16.6 %collective-permute-start.12 = (f32[704,128]{1,0:T(8,128)S(1)}, f32[704,128]{1,0:T(8,128)S(1)}, u32[]{:S(2)}, u32[]{:S(2)}) collective-permute-start(f32[704,128]{1,0:T(8,128)S(1)} %constant_dynamic-update-slice_fusion.k0), channel_id=1, source_target_pairs={{0,24},{4,28},{8,0},{12,4},{16,8},{20,12},{24,16},{28,20},{1,25},{... | collective-permute-start | bytes 1081352 | tf_op jit(solution)/shard_map/ppermute | solution.py:544
  50.0 24.5 %collective-permute-start.3 = (f32[128,512]{1,0:T(8,128)S(1)}, f32[128,512]{1,0:T(8,128)}, u32[]{:S(2)}, u32[]{:S(2)}) collective-permute-start(f32[128,512]{1,0:T(8,128)S(1)} %get-tuple-element.895), channel_id=1, source_target_pairs={{0,8},{4,12},{8,0},{12,4},{16,24},{20,28},{24,16},{28,20},{1,9},{5... | collective-permute-start | bytes 786440 | tf_op jit(solution)/shard_map/ppermute | solution.py:540
  50.8 46.4 %copy-start.10 = (f32[128,512]{1,0:T(8,128)}, f32[128,512]{1,0:T(8,128)S(1)}, u32[]{:S(2)}) copy-start(f32[128,512]{1,0:T(8,128)S(1)} %collective-permute-done.2.refs_1_) | copy-start | bytes 786436
  50.8 26.0 %collective-permute-start.4 = (f32[128,512]{1,0:T(8,128)S(1)}, f32[128,512]{1,0:T(8,128)}, u32[]{:S(2)}, u32[]{:S(2)}) collective-permute-start(f32[128,512]{1,0:T(8,128)S(1)} %get-tuple-element.895), channel_id=1, source_target_pairs={{0,12},{4,8},{8,4},{12,0},{16,28},{20,24},{24,20},{28,16},{1,13},{... | collective-permute-start | bytes 786440 | tf_op jit(solution)/shard_map/ppermute | solution.py:540
  55.7 45.0 %copy-start.7 = (f32[704,128]{1,0:T(8,128)}, f32[704,128]{1,0:T(8,128)S(1)}, u32[]{:S(2)}) copy-start(f32[704,128]{1,0:T(8,128)S(1)} %collective-permute-done.10.k1) | copy-start | bytes 1081348
  55.7 25.5 %collective-permute-start.5 = (f32[128,512]{1,0:T(8,128)S(1)}, f32[128,512]{1,0:T(8,128)}, u32[]{:S(2)}, u32[]{:S(2)}) collective-permute-start(f32[128,512]{1,0:T(8,128)S(1)} %get-tuple-element.895), channel_id=1, source_target_pairs={{0,16},{4,20},{8,24},{12,28},{16,0},{20,4},{24,8},{28,12},{1,17},{... | collective-permute-start | bytes 786440 | tf_op jit(solution)/shard_map/ppermute | solution.py:540
  64.4 1.6 %copy-start.8 = (f32[704,128]{1,0:T(8,128)}, f32[704,128]{1,0:T(8,128)S(1)}, u32[]{:S(2)}) copy-start(f32[704,128]{1,0:T(8,128)S(1)} %collective-permute-done.11.k2) | copy-start | bytes 1081348
  64.4 23.0 %collective-permute-start.6 = (f32[128,512]{1,0:T(8,128)S(1)}, f32[128,512]{1,0:T(8,128)}, u32[]{:S(2)}, u32[]{:S(2)}) collective-permute-start(f32[128,512]{1,0:T(8,128)S(1)} %get-tuple-element.895), channel_id=1, source_target_pairs={{0,20},{4,16},{8,28},{12,24},{16,4},{20,0},{24,12},{28,8},{1,21},{... | collective-permute-start | bytes 786440 | tf_op jit(solution)/shard_map/ppermute | solution.py:540
  65.9 0.7 copy-start.9
  66.7 20.7 %collective-permute-start.7 = (f32[128,512]{1,0:T(8,128)S(1)}, f32[128,512]{1,0:T(8,128)}, u32[]{:S(2)}, u32[]{:S(2)}) collective-permute-start(f32[128,512]{1,0:T(8,128)S(1)} %get-tuple-element.895), channel_id=1, source_target_pairs={{0,24},{4,28},{8,16},{12,20},{16,8},{20,12},{24,0},{28,4},{1,25},{... | collective-permute-start | bytes 786440 | tf_op jit(solution)/shard_map/ppermute | solution.py:540
  74.5 26.2 %collective-permute-start.13 = (f32[704,128]{1,0:T(8,128)S(1)}, f32[704,128]{1,0:T(8,128)}, u32[]{:S(2)}, u32[]{:S(2)}) collective-permute-start(f32[704,128]{1,0:T(8,128)S(1)} %constant_dynamic-update-slice_fusion.k0), channel_id=1, source_target_pairs={{0,4},{4,0},{8,12},{12,8},{16,20},{20,16},{24,28},{28,24},{1,5},{5... | collective-permute-start | bytes 1081352 | tf_op jit(solution)/shard_map/ppermute | solution.py:540
  76.8 23.9 %collective-permute-start.14 = (f32[704,128]{1,0:T(8,128)S(1)}, f32[704,128]{1,0:T(8,128)}, u32[]{:S(2)}, u32[]{:S(2)}) collective-permute-start(f32[704,128]{1,0:T(8,128)S(1)} %collective-permute-done.10.k1), channel_id=1, source_target_pairs={{0,4},{4,0},{8,12},{12,8},{16,20},{20,16},{24,28},{28,24},{1,5},{5... | collective-permute-start | bytes 1081352 | tf_op jit(solution)/shard_map/ppermute | solution.py:540
  81.2 19.5 %collective-permute-start.15 = (f32[704,128]{1,0:T(8,128)}, f32[704,128]{1,0:T(8,128)}, u32[]{:S(2)}, u32[]{:S(2)}) collective-permute-start(f32[704,128]{1,0:T(8,128)} %copy-done.8), channel_id=1, source_target_pairs={{0,4},{4,0},{8,12},{12,8},{16,20},{20,16},{24,28},{28,24},{1,5},{5... | collective-permute-start | bytes 1081352 | tf_op jit(solution)/shard_map/ppermute | solution.py:540
  87.4 13.4 %collective-permute-start.16 = (f32[704,128]{1,0:T(8,128)}, f32[704,128]{1,0:T(8,128)}, u32[]{:S(2)}, u32[]{:S(2)}) collective-permute-start(f32[704,128]{1,0:T(8,128)} %copy-done.9), channel_id=1, source_target_pairs={{0,4},{4,0},{8,12},{12,8},{16,20},{20,16},{24,28},{28,24},{1,5},{5... | collective-permute-start | bytes 1081352 | tf_op jit(solution)/shard_map/ppermute | solution.py:540
  87.4 9.8 %collective-permute-start.8 = (f32[128,512]{1,0:T(8,128)S(1)}, f32[128,512]{1,0:T(8,128)}, u32[]{:S(2)}, u32[]{:S(2)}) collective-permute-start(f32[128,512]{1,0:T(8,128)S(1)} %get-tuple-element.895), channel_id=1, source_target_pairs={{0,28},{4,24},{8,20},{12,16},{16,12},{20,8},{24,4},{28,0},{1,29},{... | collective-permute-start | bytes 786440 | tf_op jit(solution)/shard_map/ppermute | solution.py:540
  100.7 13.1 %copy-start.3 = (f32[512,512]{1,0:T(8,128)S(1)}, f32[512,512]{1,0:T(8,128)}, u32[]{:S(2)}) copy-start(f32[512,512]{1,0:T(8,128)} %rows_ref.3) | copy-start | bytes 3145732
where the time goes:
time: 130 us; the launch traced here: 129 us
  Pallas kernels  56.9 us (44%)
  waiting for transfers between devices  34.4 us (26%)
  starting transfers between devices  32.9 us (25%)
  local copies, waits for them, and re-layouts  2.61 us (2%)
    ppermute x12, waiting for transfers between devices, partner(): return lax.ppermute(x, 'col', [(c, c ^ by) for c in range(8)])  18 us
    pallas_call x1, Pallas kernels, slab_math(): pl.pallas_call(slab_kernel, grid=(NB // WIDE,), in_specs=[SMEM, SMEM, who...  15 us
    ppermute x12, starting transfers between devices, partner(): return lax.ppermute(x, 'col', [(c, c ^ by) for c in range(8)])  14.8 us
    pallas_call x1, Pallas kernels, panel_math(): pl.pallas_call(panel_math_kernel, in_specs=[SMEM] * 2 + [VMEM] * 3 + [ANY...  13 us
    all_to_all x2, starting transfers between devices, exchange(): lax.all_to_all(blocks.reshape(PEERS, CAP, width), RD, 0, 0)  12.4 us
    ppermute x3, waiting for transfers between devices, shift(): lax.ppermute(x, 'col', [(c, (c // 2 + by) % 4 * 2 + c % 2) for c in range...  10.9 us
    pallas_call x1, Pallas kernels, fold(): pl.pallas_call(fold_kernel, in_specs=[VMEM] * 2, out_specs=[VMEM] * 2, ou...  6.72 us
    pallas_call x1, Pallas kernels, make_plan(): pl.pallas_call(plan_kernel, in_specs=[SMEM] + [VMEM] * 3, out_specs=[VMEM...  6.06 us
  transfers between devices with their start and end apart: 17, of which 8 were waited for; matrix products, arithmetic and copies ran while one was open for 1% of the time, Pallas kernels for 28%

commit v1 on v0

--- a/solution.py
+++ b/solution.py
@@ -28,28 +28,48 @@
     return high, (x - high.astype(F32)).astype(BF16)
 
 
-def split3(x):
-    high = x.astype(BF16)
-    rest = x - high.astype(F32)
-    middle = rest.astype(BF16)
-    return high, middle, (rest - middle.astype(F32)).astype(BF16)
-
-
 def mm(a, b):
     return jnp.dot(a, b, preferred_element_type=F32)
 
 
 def dot3(a, b):
-    return mm(a[0], b[0]) + (mm(a[0], b[1]) + mm(a[1], b[0]))
+    both = jnp.concatenate([a[0], a[1]], axis=1)
+    return mm(both, jnp.concatenate([b[0], b[0]], axis=0)) + mm(a[0], b[1])
+
+
+def cut(parts, rows, cols):
+    return tuple(p[rows, cols] for p in parts)
+
+
+FIRST, LAST, ALL = slice(0, NB // 2), slice(NB // 2, NB), slice(None)
+
+
+def dot3_upper(a, b):
+    left = dot3(cut(a, ALL, FIRST), cut(b, FIRST, FIRST))
+    return jnp.concatenate([left, dot3(a, cut(b, ALL, LAST))], axis=1)
+
+
+def dot3_lower(a, b):
+    top = dot3(cut(a, FIRST, FIRST), cut(b, FIRST, ALL))
+    return jnp.concatenate([top, dot3(cut(a, LAST, ALL), b)], axis=0)
 
 
 def pick(onehot, parts):
-    return (mm(onehot, parts[0]) + mm(onehot, parts[1])) + mm(onehot, parts[2])
+    width = parts[0].shape[1]
+    if width > 128:
+        return mm(onehot, parts[0]) + mm(onehot, parts[1])
+    both = mm(onehot, jnp.concatenate(parts, axis=1))
+    return both[:, :width] + both[:, width:]
 
 
 def pick_t(onehot, parts):
-    dots = [lax.dot_general(onehot, p, (((1,), (1,)), ((), ())), preferred_element_type=F32) for p in parts]
-    return (dots[0] + dots[1]) + dots[2]
+    both = jnp.concatenate(parts, axis=0)
+    both = lax.dot_general(onehot, both, (((1,), (1,)), ((), ())), preferred_element_type=F32)
+    return both[:, :128] + both[:, 128:]
+
+
+def in_first(code):
+    return jnp.where((code & 4095) < CAP, (code >> 12) * CAP + (code & 4095), -1)
 
 
 def column(row):
@@ -72,13 +92,14 @@
 def blocks_onehot(rank, code, first, count):
     k = iota((CAP, NB), 0)
     held = k == rank
+    code = in_first(code)
     blocks = [
         jnp.where(held | ((k + (first + b) * CAP) == code), 1.0, 0.0).astype(BF16) for b in range(count)
     ]
     return jnp.concatenate(blocks, axis=0)
 
 
-def plan_kernel(where_ref, one_ref, two_ref, panel_ref, at_ref, codes_ref, every_ref, most_ref, out_ref):
+def plan_kernel(where_ref, one_ref, two_ref, panel_ref, codes_ref, every_ref, most_ref, out_ref):
     me = where_ref[0]
     one, two = one_ref[...].astype(F32), two_ref[...].astype(F32)
     one_c, two_c = column(one), column(two)
@@ -101,35 +122,26 @@
     taker_rows = jnp.concatenate([jnp.where(iota((PEERS, NB), 0) == t, 1.0, 0.0) for t in takers], axis=0)
     taker_count = taker_rows * running(taker_rows)
     most = jnp.max(rank)
-    out_codes, in_codes, out_every, in_every = [], [], [], []
+    out_codes, in_codes = [], []
     for q in range(2):
         sent = count[q:q + 1, 2 * NB - 1:]
         place = jnp.sum(taker_count[q * PEERS:(q + 1) * PEERS], axis=0, keepdims=True) - 1.0 + sent
         place = place.astype(jnp.int32)
         most = jnp.maximum(most, jnp.max(jnp.where(takers[q] < 0, 0, place).astype(F32)))
-        fits = place < CAP
-        out_codes.append(jnp.where((takers[q] >= 0) & fits, takers[q] * CAP + place, -1))
-        in_codes.append(jnp.where(fits, place + (q * CAP + 2), 1).astype(F32))
-        out_every.append(jnp.where(takers[q] >= 0, takers[q] * 4096 + place, -1))
-        in_every.append((place + (q * 4096 + 1)).astype(F32))
+        out_codes.append(jnp.where(takers[q] >= 0, takers[q] * 4096 + place, -1))
+        in_codes.append((place + (q * 4096 + 1)).astype(F32))
     most_ref[0] = most.astype(jnp.int32)
     mine = lane + (me * NB).astype(F32)
     out_rank = (down(column(source) == mine, column(rank) + 1.0) - 1.0).astype(jnp.int32)
     out_code = jnp.where(me == 0, out_codes[0], jnp.where(me == 1, out_codes[1], -1))
-    code = jnp.where(me == 0, out_every[0], jnp.where(me == 1, out_every[1], -1))
     hit = column(jnp.concatenate(leaves, axis=1)) == mine
-    in_code = down(hit, column(jnp.concatenate(in_codes, axis=1)))
-    rank = rank.astype(jnp.int32)
-    at_ref[...] = jnp.where(rank < CAP, owner * CAP + rank, -1)
+    in_code = down(hit, column(jnp.concatenate(in_codes, axis=1))).astype(jnp.int32) - 1
     codes_ref[0:1] = out_rank
     codes_ref[1:2] = out_code
-    codes_ref[2:3] = in_code.astype(jnp.int32) - 2
-    codes_ref[3:4] = code
-    codes_ref[4:5] = code
-    codes_ref[5:8] = jnp.zeros((3, NB), jnp.int32)
-    every_ref[:, :2 * NB] = owner * 4096 + rank
-    every_ref[:, 2 * NB:] = down(hit, column(jnp.concatenate(in_every, axis=1))).astype(jnp.int32) - 1
-    parts = split3(panel_ref[...])
+    codes_ref[2:8] = jnp.zeros((6, NB), jnp.int32)
+    every_ref[:, :2 * NB] = owner * 4096 + rank.astype(jnp.int32)
+    every_ref[:, 2 * NB:] = in_code
+    parts = split2(panel_ref[...])
     for c in range(4):
         onehot = blocks_onehot(out_rank, out_code, 4 * c, 4)
         out_ref[4 * c * CAP:4 * (c + 1) * CAP] = pick_t(onehot, parts)
@@ -139,9 +151,8 @@
     return pl.pallas_call(
         plan_kernel,
         in_specs=[SMEM] + [VMEM] * 3,
-        out_specs=[VMEM, VMEM, VMEM, SMEM, VMEM],
+        out_specs=[VMEM, VMEM, SMEM, VMEM],
         out_shape=[
-            jax.ShapeDtypeStruct((1, 2 * NB), jnp.int32),
             jax.ShapeDtypeStruct((8, NB), jnp.int32),
             jax.ShapeDtypeStruct((1, 3 * NB), jnp.int32),
             jax.ShapeDtypeStruct((1,), jnp.int32),
@@ -156,7 +167,7 @@
 
     @pl.when(step == 0)
     def _():
-        for n, part in enumerate(split3(rows_ref[...])):
+        for n, part in enumerate(split2(rows_ref[...])):
             parts_ref[n] = part
 
     onehot = blocks_onehot(codes_ref[0:1], codes_ref[1:2], step * 4, 4)
@@ -177,13 +188,14 @@
 
 
 def slots_of(at_ref, n):
-    at = column(at_ref[:, n * NB:(n + 1) * NB])
+    at = column(in_first(at_ref[:, n * NB:(n + 1) * NB]))
     return jnp.where(iota((NB, SLOTS), 1) == at, 1.0, 0.0).astype(BF16)
 
 
-def arrivals(codes_ref):
-    code = column(codes_ref[2:3])
-    return jnp.where(iota((NB, 2 * CAP), 1) == code, 1.0, 0.0).astype(BF16), code > -2
+def arrivals(at_ref):
+    code = at_ref[:, 2 * NB:]
+    at = column(in_first(code))
+    return jnp.where(iota((NB, 2 * CAP), 1) == at, 1.0, 0.0).astype(BF16), column(code) >= 0
 
 
 def late(flag_ref, extra_ref, buffer, sem):
@@ -203,7 +215,7 @@
 def panel_rows_kernel(where_ref, flag_ref, at_ref, got_ref, extra_ref, keep_ref, send_ref, tops_ref, more, sem):
     core = where_ref[1]
     more = late(flag_ref, extra_ref.at[:2 * NB, :128], more, sem)
-    parts = split3(got_ref[...])
+    parts = split2(got_ref[...])
     first = pick(slots_of(at_ref, 0), parts) + more[:NB]
     second = pick(slots_of(at_ref, 1), parts) + more[NB:]
     left = iota((NB, 128), 1) < 64
@@ -242,28 +254,29 @@
     )(at, lower_inv)
 
 
-def own_panels_kernel(where_ref, *refs):
-    pieces, out_ref, gath = refs[:8], refs[8], refs[9]
-    col = where_ref[3]
-    for m in range(8):
-        gath[lax.bitwise_xor(col, m)] = pieces[m][...]
+def own_panels_kernel(where_ref, p0, p1, p2, p3, out_ref, gath):
+    core, z = where_ref[1], where_ref[2]
+    for s, piece in enumerate((p0, p1, p2, p3)):
+        zz = lax.rem(z + 4 - s, 4)
+        gath[zz, core] = piece[:128]
+        gath[zz, 1 - core] = piece[128:]
     for n in range(2):
-        whole = jnp.concatenate([gath[c, 64 * n:64 * (n + 1)] for c in range(8)], axis=0)
-        out_ref[n] = jnp.transpose(whole)
+        half = [gath[c // 2, c % 2, 64 * n:64 * (n + 1)] for c in range(8)]
+        out_ref[n] = jnp.transpose(jnp.concatenate(half, axis=0))
 
 
 def own_panels(where, pieces):
     return pl.pallas_call(
         own_panels_kernel,
-        in_specs=[SMEM] + [VMEM] * 8,
+        in_specs=[SMEM] + [VMEM] * 4,
         out_specs=VMEM,
         out_shape=jax.ShapeDtypeStruct((2, NB, NB), F32),
-        scratch_shapes=[pltpu.VMEM((8, 128, NB), F32)],
+        scratch_shapes=[pltpu.VMEM((4, 2, 128, NB), F32)],
         name="own_panels",
     )(where, *pieces)
 
 
-def panel_math_kernel(where_ref, flag_ref, codes_ref, tops_ref, whole_ref, extra_ref, k0, k1, k2, k3, p0, p1, p2, p3,
+def panel_math_kernel(where_ref, flag_ref, at_ref, tops_ref, whole_ref, extra_ref, k0, k1, k2, k3, p0, p1, p2, p3,
                       lower_ref, upper_ref, left_ref, pout_ref, gath, src, more, sem):
     me, core, z = where_ref[0], where_ref[1], where_ref[2]
     for s, (a, b) in enumerate(((k0, p0), (k1, p1), (k2, p2), (k3, p3))):
@@ -279,22 +292,22 @@
         ones.append(jnp.where(left, a, pltpu.roll(b, 64, 1)))
         twos.append(jnp.where(left, pltpu.roll(a, 64, 1), b))
     in_one, in_two = jnp.concatenate(ones, axis=1), jnp.concatenate(twos, axis=1)
-    onehot, moved = arrivals(codes_ref)
+    onehot, moved = arrivals(at_ref)
     top_two_one, top_one_two = in_one[:NB], in_two[:NB]
-    own_one = jnp.where(moved, pick(onehot, split3(in_one[NB:])) + more[0], whole_ref[0])
-    own_two = jnp.where(moved, pick(onehot, split3(in_two[NB:])) + more[1], whole_ref[1])
+    own_one = jnp.where(moved, pick(onehot, split2(in_one[NB:])) + more[0], whole_ref[0])
+    own_two = jnp.where(moved, pick(onehot, split2(in_two[NB:])) + more[1], whole_ref[1])
     own_one = jnp.where(me == 1, top_two_one, own_one)
     own_two = jnp.where(me == 1, 0.0, own_two)
     upper_one_inv = split2(upper_ref[0])
-    lower_kept = dot3(split2(own_one), upper_one_inv)
-    lower_top = dot3(split2(top_two_one), upper_one_inv)
-    upper_panel = dot3(split2(lower_ref[0]), split2(top_one_two))
+    lower_kept = dot3_upper(split2(own_one), upper_one_inv)
+    lower_top = dot3_upper(split2(top_two_one), upper_one_inv)
+    upper_panel = dot3_lower(split2(lower_ref[0]), split2(top_one_two))
     kept_parts = split2(lower_kept)
     updated = own_two - dot3(kept_parts, split2(upper_panel))
-    lower_two = dot3(split2(updated), split2(upper_ref[1]))
+    lower_two = dot3_upper(split2(updated), split2(upper_ref[1]))
     left_ref[0], left_ref[1] = kept_parts
     left_ref[2], left_ref[3] = split2(lower_two)
-    left_ref[4], left_ref[5] = split2(dot3(split2(lower_ref[1]), split2(lower_top)))
+    left_ref[4], left_ref[5] = split2(dot3_lower(split2(lower_ref[1]), split2(lower_top)))
     src[0] = lower_kept
     src[1] = jnp.where(me == 0, upper_panel, jnp.where(me == 1, updated, lower_two))
     at = pl.multiple_of(z * 128, 128)
@@ -312,7 +325,7 @@
     pout_ref[...] = jnp.transpose(mine)
 
 
-def panel_math(where, flag, codes, tops, whole, extra, kept, other, lower_inv, upper_inv):
+def panel_math(where, flag, at, tops, whole, extra, kept, other, lower_inv, upper_inv):
     return pl.pallas_call(
         panel_math_kernel,
         in_specs=[SMEM] * 2 + [VMEM] * 3 + [ANY] + [VMEM] * 10,
@@ -325,13 +338,13 @@
             pltpu.SemaphoreType.DMA,
         ],
         name="panel_math",
-    )(where, flag, codes, tops, whole, extra, *kept, *other, lower_inv, upper_inv)
+    )(where, flag, at, tops, whole, extra, *kept, *other, lower_inv, upper_inv)
 
 
 WIDE = 256
 
 
-def slab_kernel(where_ref, flag_ref, codes_ref, got_ref, rows_ref, extra_ref, one_ref, two_ref, left_ref, out_ref,
+def slab_kernel(where_ref, flag_ref, at_ref, got_ref, rows_ref, extra_ref, one_ref, two_ref, left_ref, out_ref,
                 more, sem):
     me = where_ref[0]
     at = pl.multiple_of(pl.program_id(0) * WIDE, WIDE)
@@ -351,13 +364,13 @@
 
     @pl.when(me > 1)
     def _():
-        onehot, moved = arrivals(codes_ref)
-        own = jnp.where(moved, pick(onehot, split3(got_ref[:2 * CAP])) + more[2 * NB:], rows_ref[...])
+        onehot, moved = arrivals(at_ref)
+        own = jnp.where(moved, pick(onehot, split2(got_ref[:2 * CAP])) + more[2 * NB:], rows_ref[...])
         two = split2(upper_two)
         out_ref[...] = own - dot3((left_ref[0], left_ref[1]), one) - dot3((left_ref[2], left_ref[3]), two)
 
 
-def slab_math(where, flag, codes, got, rows, extra, one, two, left):
+def slab_math(where, flag, at, got, rows, extra, one, two, left):
     whole = lambda *shape: pl.BlockSpec(shape, lambda i: (0,) * len(shape))
     return pl.pallas_call(
         slab_kernel,
@@ -365,7 +378,7 @@
         in_specs=[
             SMEM,
             SMEM,
-            whole(8, NB),
+            whole(1, 3 * NB),
             pl.BlockSpec((SLOTS, WIDE), lambda i: (0, i)),
             pl.BlockSpec((NB, WIDE), lambda i: (0, i)),
             ANY,
@@ -377,7 +390,7 @@
         out_shape=jax.ShapeDtypeStruct((NB, NB), F32),
         scratch_shapes=[pltpu.VMEM((3 * NB, WIDE), F32), pltpu.SemaphoreType.DMA],
         name="slab_math",
-    )(where, flag, codes, got, rows, extra, one, two, left)
+    )(where, flag, at, got, rows, extra, one, two, left)
 
 
 def mark_kernel(in_ref, out_ref):
@@ -410,10 +423,10 @@
 
 def late_pack_kernel(base_ref, codes_ref, panel_ref, rows_ref, out_ref):
     k = iota((CAP, NB), 0) + base_ref[0]
-    picked = (k == codes_ref[0:1]) | ((k + pl.program_id(0) * 4096) == codes_ref[4:5])
+    picked = (k == codes_ref[0:1]) | ((k + pl.program_id(0) * 4096) == codes_ref[1:2])
     onehot = jnp.where(picked, 1.0, 0.0).astype(BF16)
-    out_ref[:, :128] = pick_t(onehot, split3(panel_ref[...]))
-    out_ref[:, 128:] = pick(onehot, split3(rows_ref[...]))
+    out_ref[:, :128] = pick_t(onehot, split2(panel_ref[...]))
+    out_ref[:, 128:] = pick(onehot, split2(rows_ref[...]))
 
 
 def late_pack(base, codes, panel_t, slab):
@@ -435,7 +448,7 @@
     at = jnp.where(now, (code >> 12) * CAP + place, -1)
     onehot = jnp.where(iota((128, SLOTS), 1) == at, 1.0, 0.0).astype(BF16)
     old = jnp.where(base_ref[0] == CAP, 0.0, old_ref[...])
-    out_ref[...] = jnp.where(now, pick(onehot, split3(got_ref[...])), old)
+    out_ref[...] = jnp.where(now, pick(onehot, split2(got_ref[...])), old)
 
 
 def late_place(base, every, got, old):
@@ -536,8 +549,8 @@
     return lax.while_loop(lambda s: s[0] * CAP <= most, turn, start)[1:]
 
 
-def partner(x, by=1):
-    return lax.ppermute(x, "col", [(c, c ^ by) for c in range(8)])
+def partner(x):
+    return lax.ppermute(x, "col", [(c, c ^ 1) for c in range(8)])
 
 
 def shift(x, by):
@@ -549,23 +562,24 @@
     col = lax.axis_index("col")
     where = jnp.stack([me, col % 2, col // 2, col]).astype(jnp.int32)
     panel_t = jnp.swapaxes(panels, 1, 2).reshape(128, NB)
-    at, codes, every, most, blocks = make_plan(where, pivot_one, pivot_two, panel_t)
+    panel_pair = jnp.concatenate([panel_t, partner(panel_t)], axis=0)
+    codes, every, most, blocks = make_plan(where, pivot_one, pivot_two, panel_t)
     got_panel = exchange(blocks)
-    pieces = [panel_t] + [partner(panel_t, by) for by in range(1, 8)]
+    pieces = [panel_pair] + [shift(panel_pair, by) for by in (1, 2, 3)]
     whole = own_panels(where, pieces)
     blocks = pack(codes, slab)
     most = mark(most)
     late_rows, late_own, late_slab = further_rounds(most[0], codes, every, panel_t, slab, lower_inv, me, col)
     got_slab = exchange(blocks)
-    keep, send, tops = panel_rows(where, most, at, got_panel, late_rows)
+    keep, send, tops = panel_rows(where, most, every, got_panel, late_rows)
     pair = jnp.concatenate([keep, partner(send)], axis=0)
     shifted = [shift(pair, by) for by in (1, 2, 3)]
-    one, two = fold(at, lower_inv)
+    one, two = fold(every, lower_inv)
     shifted, one, two = lax.optimization_barrier((shifted, one, two))
     kept = [pair] + shifted
     other = [partner(x) for x in kept]
-    left, panel_out = panel_math(where, most, codes, tops, whole, late_own, kept, other, lower_inv, upper_inv)
-    slab_out = slab_math(where, most, codes, got_slab, slab, late_slab, one, two, left)
+    left, panel_out = panel_math(where, most, every, tops, whole, late_own, kept, other, lower_inv, upper_inv)
+    slab_out = slab_math(where, most, every, got_slab, slab, late_slab, one, two, left)
     return jnp.swapaxes(panel_out.reshape(2, 64, NB), 1, 2), slab_out
 
 

time: 130 us -> 118 us (0.908)
  starting transfers between devices: 32.9 us -> 26.2 us
  Pallas kernels: 56.9 us -> 51.7 us
    ppermute x12 -> x6, waiting for transfers between devices: 18 us -> 0.02 us  [partner(): return lax.ppermute(x, 'col', [(c, c ^ 1) for c in range(8)])]
    ppermute x3 -> x6, waiting for transfers between devices: 10.9 us -> 28.4 us  [shift(): lax.ppermute(x, 'col', [(c, (c // 2 + by) % 4 * 2 + c % 2) for c in range...]
    ppermute x12 -> x6, starting transfers between devices: 14.8 us -> 5.31 us  [partner(): return lax.ppermute(x, 'col', [(c, c ^ 1) for c in range(8)])]
    ppermute x3 -> x6, starting transfers between devices: 5.74 us -> 8.53 us  [shift(): lax.ppermute(x, 'col', [(c, (c // 2 + by) % 4 * 2 + c % 2) for c in range...]
    pallas_call x1, Pallas kernels: 5.87 us -> 4.13 us  [panel_rows(): pl.pallas_call(panel_rows_kernel, in_specs=[SMEM] * 2 + [VMEM] * 2 + [ANY...]
    unnamed x21 -> x17, local copies, waits for them, and re-layouts: 2.6 us -> 2.81 us
  transfers between devices with their start and end apart: 17 -> 14, of which waited for: 8 -> 3; matrix products, arithmetic and copies ran while one was open for 1% -> 2% of each run, Pallas kernels for 28% -> 27%
where the time goes in v1:
time: 118 us; the launch traced here: 117 us
  Pallas kernels  51.7 us (44%)
  waiting for transfers between devices  33.4 us (28%)
  starting transfers between devices  26.2 us (22%)
  local copies, waits for them, and re-layouts  2.82 us (2%)
  other arithmetic  1.64 us (1%)
    ppermute x6, waiting for transfers between devices, shift(): lax.ppermute(x, 'col', [(c, (c // 2 + by) % 4 * 2 + c % 2) for c in range...  28.4 us
    pallas_call x1, Pallas kernels, slab_math(): pl.pallas_call(slab_kernel, grid=(NB // WIDE,), in_specs=[SMEM, SMEM, who...  15 us
    all_to_all x2, starting transfers between devices, exchange(): lax.all_to_all(blocks.reshape(PEERS, CAP, width), RD, 0, 0)  12.4 us
    pallas_call x1, Pallas kernels, panel_math(): pl.pallas_call(panel_math_kernel, in_specs=[SMEM] * 2 + [VMEM] * 3 + [ANY...  11.8 us
    ppermute x6, starting transfers between devices, shift(): lax.ppermute(x, 'col', [(c, (c // 2 + by) % 4 * 2 + c % 2) for c in range...  8.53 us
    pallas_call x1, Pallas kernels, fold(): pl.pallas_call(fold_kernel, in_specs=[VMEM] * 2, out_specs=[VMEM] * 2, ou...  6.05 us
    ppermute x6, starting transfers between devices, partner(): return lax.ppermute(x, 'col', [(c, c ^ 1) for c in range(8)])  5.31 us
    pallas_call x1, Pallas kernels, make_plan(): pl.pallas_call(plan_kernel, in_specs=[SMEM] + [VMEM] * 3, out_specs=[VMEM...  5.09 us
  transfers between devices with their start and end apart: 14, of which 3 were waited for; matrix products, arithmetic and copies ran while one was open for 2% of the time, Pallas kernels for 27%

profile of v1, /device:TPU:5, one launch (start us, length us, event | category | flops | bytes accessed | tf_op | source)
XLA Modules:
  0.0 117.4 jit_solution(7778514362144062566)
XLA Ops:
  0.7 0.7 pad_add_fusion.where_ref
  1.3 5.1 %make_plan.1 = (s32[8,512]{1,0:T(8,128)S(1)}, s32[1,1536]{1,0:T(1,128)S(1)}, s32[1]{0:T(128)}, f32[1536,128]{1,0:T(8,128)}) custom-call(s32[4]{0:T(128)} %pad_add_fusion.where_ref, s32[1,512]{1,0:T(1,128)} %bitcast.30, s32[1,512]{1,0:T(1,128)} %bitcast.31, f32[128,512]{1,0:T(8,128)} %bitcast.24), custom_call_target="tpu_custom_call" | custom-call | tf_op jit(solution)/shard_map/make_plan/pallas_call | solution.py:151
  6.4 6.9 %all-to-all-start = ((f32[16,96,128]{2,1,0:T(8,128)}), f32[16,96,128]{2,1,0:T(8,128)S(1)}, u32[]{:S(2)}, u32[]{:S(2)}) async-start(f32[16,96,128]{2,1,0:T(8,128)} %bitcast.29), calls=%async_computation | async-start | bytes 1572864 | tf_op jit(solution)/shard_map/all_to_all | solution.py:408
  13.3 1.2 %collective-permute-start.2 = (f32[128,512]{1,0:T(8,128)}, f32[128,512]{1,0:T(8,128)}, u32[]{:S(2)}, u32[]{:S(2)}) collective-permute-start(f32[128,512]{1,0:T(8,128)} %bitcast.25), channel_id=1, source_target_pairs={{0,4},{4,0},{8,12},{12,8},{16,20},{20,16},{24,28},{28,24},{1,5},{5... | collective-permute-start | bytes 786440 | tf_op jit(solution)/shard_map/ppermute | solution.py:553
  14.5 1.1 mark.1.flag_ref
  15.6 5.0 %pack_rows.1 = f32[1536,512]{1,0:T(8,128)} custom-call(s32[8,512]{1,0:T(8,128)S(1)} %get-tuple-element.808.codes_ref, f32[512,512]{1,0:T(8,128)} %rows_ref.3), custom_call_target="tpu_custom_call" | custom-call | tf_op jit(solution)/shard_map/pack_rows/pallas_call | solution.py:179
  20.6 4.9 %all-to-all-done = f32[16,96,128]{2,1,0:T(8,128)S(1)} async-done(((f32[16,96,128]{2,1,0:T(8,128)}), f32[16,96,128]{2,1,0:T(8,128)S(1)}, u32[]{:S(2)}, u32[]{:S(2)}) %all-to-all-start) | async-done | bytes 786464 | tf_op jit(solution)/shard_map/all_to_all | solution.py:408
  25.5 0.9 copy-done.5
  26.4 5.5 %all-to-all-start.1 = ((f32[16,96,512]{2,1,0:T(8,128)}), f32[16,96,512]{2,1,0:T(8,128)}, u32[]{:S(2)}, u32[]{:S(2)}) async-start(f32[16,96,512]{2,1,0:T(8,128)} %bitcast.27), calls=%async_computation.1 | async-start | bytes 6291456 | tf_op jit(solution)/shard_map/all_to_all | solution.py:408
  31.9 0.0 copy-done.1
  31.9 0.0 copy-done.4
  31.9 0.6 while.66
  32.5 0.0 copy-start
  32.6 4.1 %panel_rows.1 = (f32[352,128]{1,0:T(8,128)}, f32[352,128]{1,0:T(8,128)}, f32[512,128]{1,0:T(8,128)}) custom-call(s32[4]{0:T(128)} %pad_add_fusion.where_ref, s32[1]{0:T(128)} %mark.1.flag_ref, s32[1,1536]{1,0:T(1,128)S(1)} %get-tuple-element.897, f32[1536,128]{1,0:T(8,128)} %bitcast.28, f32[1536,640]{1,0:T(8,128)} %get-tuple-element.888), custom_call_target="tpu_custom_call" | custom-call | tf_op jit(solution)/shard_map/panel_rows/pallas_call | solution.py:232
  36.7 2.6 %collective-permute-start.6 = (f32[352,128]{1,0:T(8,128)}, f32[352,128]{1,0:T(8,128)S(1)}, u32[]{:S(2)}, u32[]{:S(2)}) collective-permute-start(f32[352,128]{1,0:T(8,128)} %get-tuple-element.536), channel_id=1, source_target_pairs={{0,4},{4,0},{8,12},{12,8},{16,20},{20,16},{24,28},{28,24},{1,5},{5... | collective-permute-start | bytes 540680 | tf_op jit(solution)/shard_map/ppermute | solution.py:553
  39.3 0.0 collective-permute-done.2
  39.3 1.0 pad_maximum_fusion.p0
  40.3 0.0 copy-start.6
  40.3 1.1 constant_dynamic-update-slice_fusion.1
  41.4 0.0 collective-permute-done.6
  41.5 1.7 %collective-permute-start.7 = (f32[704,128]{1,0:T(8,128)S(1)}, f32[704,128]{1,0:T(8,128)S(1)}, u32[]{:S(2)}, u32[]{:S(2)}) collective-permute-start(f32[704,128]{1,0:T(8,128)S(1)} %constant_dynamic-update-slice_fusion.k0), channel_id=1, source_target_pairs={{0,8},{4,12},{8,16},{12,20},{16,24},{20,28},{24,0},{28,4},{1,9},{5... | collective-permute-start | bytes 1081352 | tf_op jit(solution)/shard_map/ppermute | solution.py:557
  43.2 1.6 %collective-permute-start.3 = (f32[256,512]{1,0:T(8,128)S(1)}, f32[256,512]{1,0:T(8,128)}, u32[]{:S(2)}, u32[]{:S(2)}) collective-permute-start(f32[256,512]{1,0:T(8,128)S(1)} %pad_maximum_fusion.p0), channel_id=1, source_target_pairs={{0,8},{4,12},{8,16},{12,20},{16,24},{20,28},{24,0},{28,4},{1,9},{5... | collective-permute-start | bytes 1572872 | tf_op jit(solution)/shard_map/ppermute | solution.py:557
  44.8 1.7 %collective-permute-start.4 = (f32[256,512]{1,0:T(8,128)S(1)}, f32[256,512]{1,0:T(8,128)}, u32[]{:S(2)}, u32[]{:S(2)}) collective-permute-start(f32[256,512]{1,0:T(8,128)S(1)} %pad_maximum_fusion.p0), channel_id=1, source_target_pairs={{0,16},{4,20},{8,24},{12,28},{16,0},{20,4},{24,8},{28,12},{1,17},{... | collective-permute-start | bytes 1572872 | tf_op jit(solution)/shard_map/ppermute | solution.py:557
  46.6 1.2 %collective-permute-start.8 = (f32[704,128]{1,0:T(8,128)S(1)}, f32[704,128]{1,0:T(8,128)}, u32[]{:S(2)}, u32[]{:S(2)}) collective-permute-start(f32[704,128]{1,0:T(8,128)S(1)} %constant_dynamic-update-slice_fusion.k0), channel_id=1, source_target_pairs={{0,16},{4,20},{8,24},{12,28},{16,0},{20,4},{24,8},{28,12},{1,17},{... | collective-permute-start | bytes 1081352 | tf_op jit(solution)/shard_map/ppermute | solution.py:557
  47.8 1.0 collective-permute-start.9
  48.8 5.3 %collective-permute-done.7.k1 = f32[704,128]{1,0:T(8,128)S(1)} collective-permute-done((f32[704,128]{1,0:T(8,128)S(1)}, f32[704,128]{1,0:T(8,128)S(1)}, u32[]{:S(2)}, u32[]{:S(2)}) %collective-permute-start.7) | collective-permute-done | bytes 360480 | tf_op jit(solution)/shard_map/ppermute | solution.py:557
  54.2 0.8 copy-done.8
  55.0 1.2 %collective-permute-start.5 = (f32[256,512]{1,0:T(8,128)S(1)}, f32[256,512]{1,0:T(8,128)}, u32[]{:S(2)}, u32[]{:S(2)}) collective-permute-start(f32[256,512]{1,0:T(8,128)S(1)} %pad_maximum_fusion.p0), channel_id=1, source_target_pairs={{0,24},{4,28},{8,0},{12,4},{16,8},{20,12},{24,16},{28,20},{1,25},{... | collective-permute-start | bytes 1572872 | tf_op jit(solution)/shard_map/ppermute | solution.py:557
  56.1 6.0 %fold_slots.1 = (bf16[2,512,1536]{2,1,0:T(8,128)(2,1)}, bf16[2,512,1536]{2,1,0:T(8,128)(2,1)}) custom-call(s32[1,1536]{1,0:T(1,128)S(1)} %get-tuple-element.897, f32[2,512,512]{2,1,0:T(8,128)S(1)} %copy-done), custom_call_target="tpu_custom_call" | custom-call | tf_op jit(solution)/shard_map/fold_slots/pallas_call | solution.py:252
  62.2 23.1 %collective-permute-done.8.k2 = f32[704,128]{1,0:T(8,128)} collective-permute-done((f32[704,128]{1,0:T(8,128)S(1)}, f32[704,128]{1,0:T(8,128)}, u32[]{:S(2)}, u32[]{:S(2)}) %collective-permute-start.8) | collective-permute-done | bytes 360480 | tf_op jit(solution)/shard_map/ppermute | solution.py:557
  85.3 0.9 collective-permute-start.10
  86.1 0.0 collective-permute-done.9.k3
  86.2 0.0 collective-permute-start.11
  86.2 0.0 collective-permute-done.3.p1
  86.2 0.5 collective-permute-start.12
  86.7 0.0 collective-permute-done.4.p2
  86.7 0.1 collective-permute-start.13
  86.8 0.0 collective-permute-done.5.p3
  86.8 3.6 %own_panels.1.whole_ref = f32[2,512,512]{2,1,0:T(8,128)} custom-call(s32[4]{0:T(128)} %pad_add_fusion.where_ref, f32[256,512]{1,0:T(8,128)} %copy-done.6, f32[256,512]{1,0:T(8,128)} %collective-permute-done.3.p1, f32[256,512]{1,0:T(8,128)} %collective-permute-done.4.p2, f32[256,512]{1,0:T(8,128)} %collective-permute-done.5.p3), custom_call_target="tpu_custom_call" | custom-call | tf_op jit(solution)/shard_map/own_panels/pallas_call | solution.py:269
  90.3 0.0 copy-done.7
  90.3 0.0 collective-permute-done.10.p0
  90.3 0.0 collective-permute-done.11.p1
  90.4 0.0 collective-permute-done.12.p2
  90.4 0.0 collective-permute-done.13.p3
  90.4 0.0 copy-start.3
  90.4 11.8 %panel_math.1 = (bf16[6,512,512]{2,1,0:T(8,128)(2,1)}, f32[128,512]{1,0:T(8,128)}) custom-call(s32[4]{0:T(128)} %pad_add_fusion.where_ref, s32[1]{0:T(128)} %mark.1.flag_ref, s32[1,1536]{1,0:T(1,128)S(1)} %get-tuple-element.897, f32[512,128]{1,0:T(8,128)} %get-tuple-element.533.tops_ref, f32[2,512,512]{2,1,0:T(8,128)} %own_panels.1.whole_ref, ...), custom_call_target="tpu_custom_call" | custom-call | tf_op jit(solution)/shard_map/panel_math/pallas_call | solution.py:329
  102.2 0.0 all-to-all-done.1
  102.3 15.0 %slab_math.1 = f32[512,512]{1,0:T(8,128)} custom-call(s32[4]{0:T(128)} %pad_add_fusion.where_ref, s32[1]{0:T(128)} %mark.1.flag_ref, s32[1,1536]{1,0:T(1,128)S(1)} %get-tuple-element.897, f32[1536,512]{1,0:T(8,128)} %bitcast.17.got_ref, f32[512,512]{1,0:T(8,128)S(1)} %copy-done.3, f32[1536,512]{1,0:T(8,128)} %get-tuple-element.890, ...), custom_call_target="tpu_custom_call" | custom-call | tf_op jit(solution)/shard_map/slab_math/pallas_call | solution.py:375
  (10 shorter events, 0.0 us)
Async XLA Ops:
  6.4 19.1 %all-to-all-start = ((f32[16,96,128]{2,1,0:T(8,128)}), f32[16,96,128]{2,1,0:T(8,128)S(1)}, u32[]{:S(2)}, u32[]{:S(2)}) async-start(f32[16,96,128]{2,1,0:T(8,128)} %bitcast.29), calls=%async_computation | async-start | bytes 1572864 | tf_op jit(solution)/shard_map/all_to_all | solution.py:408
  13.3 26.0 %collective-permute-start.2 = (f32[128,512]{1,0:T(8,128)}, f32[128,512]{1,0:T(8,128)}, u32[]{:S(2)}, u32[]{:S(2)}) collective-permute-start(f32[128,512]{1,0:T(8,128)} %bitcast.25), channel_id=1, source_target_pairs={{0,4},{4,0},{8,12},{12,8},{16,20},{20,16},{24,28},{28,24},{1,5},{5... | collective-permute-start | bytes 786440 | tf_op jit(solution)/shard_map/ppermute | solution.py:553
  25.5 0.9 copy-start.5
  26.4 5.5 %copy-start.1 = (f32[512,512]{1,0:T(8,128)S(1)}, f32[512,512]{1,0:T(8,128)}, u32[]{:S(2)}) copy-start(f32[512,512]{1,0:T(8,128)} %rows_ref.3) | copy-start | bytes 3145732
  26.4 5.5 %copy-start.4 = (f32[2,512,64]{1,2,0:T(8,128)S(1)}, f32[2,512,64]{1,2,0:T(8,128)}, u32[]{:S(2)}) copy-start(f32[2,512,64]{1,2,0:T(8,128)} %param.12) | copy-start | bytes 786436
  26.4 75.8 %all-to-all-start.1 = ((f32[16,96,512]{2,1,0:T(8,128)}), f32[16,96,512]{2,1,0:T(8,128)}, u32[]{:S(2)}, u32[]{:S(2)}) async-start(f32[16,96,512]{2,1,0:T(8,128)} %bitcast.27), calls=%async_computation.1 | async-start | bytes 6291456 | tf_op jit(solution)/shard_map/all_to_all | solution.py:408
  32.5 23.6 %copy-start = (f32[2,512,512]{2,1,0:T(8,128)S(1)}, f32[2,512,512]{2,1,0:T(8,128)}, u32[]{:S(2)}) copy-start(f32[2,512,512]{2,1,0:T(8,128)} %get-tuple-element.899) | copy-start | bytes 6291460
  36.7 4.7 %collective-permute-start.6 = (f32[352,128]{1,0:T(8,128)}, f32[352,128]{1,0:T(8,128)S(1)}, u32[]{:S(2)}, u32[]{:S(2)}) collective-permute-start(f32[352,128]{1,0:T(8,128)} %get-tuple-element.536), channel_id=1, source_target_pairs={{0,4},{4,0},{8,12},{12,8},{16,20},{20,16},{24,28},{28,24},{1,5},{5... | collective-permute-start | bytes 540680 | tf_op jit(solution)/shard_map/ppermute | solution.py:553
  40.3 46.5 %copy-start.6 = (f32[256,512]{1,0:T(8,128)}, f32[256,512]{1,0:T(8,128)S(1)}, u32[]{:S(2)}) copy-start(f32[256,512]{1,0:T(8,128)S(1)} %pad_maximum_fusion.p0) | copy-start | bytes 1572868
  41.5 48.9 %copy-start.7 = (f32[704,128]{1,0:T(8,128)}, f32[704,128]{1,0:T(8,128)S(1)}, u32[]{:S(2)}) copy-start(f32[704,128]{1,0:T(8,128)S(1)} %constant_dynamic-update-slice_fusion.k0) | copy-start | bytes 1081348
  41.5 12.7 %collective-permute-start.7 = (f32[704,128]{1,0:T(8,128)S(1)}, f32[704,128]{1,0:T(8,128)S(1)}, u32[]{:S(2)}, u32[]{:S(2)}) collective-permute-start(f32[704,128]{1,0:T(8,128)S(1)} %constant_dynamic-update-slice_fusion.k0), channel_id=1, source_target_pairs={{0,8},{4,12},{8,16},{12,20},{16,24},{20,28},{24,0},{28,4},{1,9},{5... | collective-permute-start | bytes 1081352 | tf_op jit(solution)/shard_map/ppermute | solution.py:557
  43.2 43.0 %collective-permute-start.3 = (f32[256,512]{1,0:T(8,128)S(1)}, f32[256,512]{1,0:T(8,128)}, u32[]{:S(2)}, u32[]{:S(2)}) collective-permute-start(f32[256,512]{1,0:T(8,128)S(1)} %pad_maximum_fusion.p0), channel_id=1, source_target_pairs={{0,8},{4,12},{8,16},{12,20},{16,24},{20,28},{24,0},{28,4},{1,9},{5... | collective-permute-start | bytes 1572872 | tf_op jit(solution)/shard_map/ppermute | solution.py:557
  44.8 41.8 %collective-permute-start.4 = (f32[256,512]{1,0:T(8,128)S(1)}, f32[256,512]{1,0:T(8,128)}, u32[]{:S(2)}, u32[]{:S(2)}) collective-permute-start(f32[256,512]{1,0:T(8,128)S(1)} %pad_maximum_fusion.p0), channel_id=1, source_target_pairs={{0,16},{4,20},{8,24},{12,28},{16,0},{20,4},{24,8},{28,12},{1,17},{... | collective-permute-start | bytes 1572872 | tf_op jit(solution)/shard_map/ppermute | solution.py:557
  46.6 38.7 %collective-permute-start.8 = (f32[704,128]{1,0:T(8,128)S(1)}, f32[704,128]{1,0:T(8,128)}, u32[]{:S(2)}, u32[]{:S(2)}) collective-permute-start(f32[704,128]{1,0:T(8,128)S(1)} %constant_dynamic-update-slice_fusion.k0), channel_id=1, source_target_pairs={{0,16},{4,20},{8,24},{12,28},{16,0},{20,4},{24,8},{28,12},{1,17},{... | collective-permute-start | bytes 1081352 | tf_op jit(solution)/shard_map/ppermute | solution.py:557
  47.8 38.4 %collective-permute-start.9 = (f32[704,128]{1,0:T(8,128)S(1)}, f32[704,128]{1,0:T(8,128)}, u32[]{:S(2)}, u32[]{:S(2)}) collective-permute-start(f32[704,128]{1,0:T(8,128)S(1)} %constant_dynamic-update-slice_fusion.k0), channel_id=1, source_target_pairs={{0,24},{4,28},{8,0},{12,4},{16,8},{20,12},{24,16},{28,20},{1,25},{... | collective-permute-start | bytes 1081352 | tf_op jit(solution)/shard_map/ppermute | solution.py:557
  54.2 0.8 copy-start.8
  55.0 31.8 %collective-permute-start.5 = (f32[256,512]{1,0:T(8,128)S(1)}, f32[256,512]{1,0:T(8,128)}, u32[]{:S(2)}, u32[]{:S(2)}) collective-permute-start(f32[256,512]{1,0:T(8,128)S(1)} %pad_maximum_fusion.p0), channel_id=1, source_target_pairs={{0,24},{4,28},{8,0},{12,4},{16,8},{20,12},{24,16},{28,20},{1,25},{... | collective-permute-start | bytes 1572872 | tf_op jit(solution)/shard_map/ppermute | solution.py:557
  85.3 5.1 %collective-permute-start.10 = (f32[704,128]{1,0:T(8,128)S(1)}, f32[704,128]{1,0:T(8,128)}, u32[]{:S(2)}, u32[]{:S(2)}) collective-permute-start(f32[704,128]{1,0:T(8,128)S(1)} %constant_dynamic-update-slice_fusion.k0), channel_id=1, source_target_pairs={{0,4},{4,0},{8,12},{12,8},{16,20},{20,16},{24,28},{28,24},{1,5},{5... | collective-permute-start | bytes 1081352 | tf_op jit(solution)/shard_map/ppermute | solution.py:553
  86.2 4.2 %collective-permute-start.11 = (f32[704,128]{1,0:T(8,128)}, f32[704,128]{1,0:T(8,128)}, u32[]{:S(2)}, u32[]{:S(2)}) collective-permute-start(f32[704,128]{1,0:T(8,128)} %copy-done.8), channel_id=1, source_target_pairs={{0,4},{4,0},{8,12},{12,8},{16,20},{20,16},{24,28},{28,24},{1,5},{5... | collective-permute-start | bytes 1081352 | tf_op jit(solution)/shard_map/ppermute | solution.py:553
  86.2 4.2 %collective-permute-start.12 = (f32[704,128]{1,0:T(8,128)}, f32[704,128]{1,0:T(8,128)}, u32[]{:S(2)}, u32[]{:S(2)}) collective-permute-start(f32[704,128]{1,0:T(8,128)} %collective-permute-done.8.k2), channel_id=1, source_target_pairs={{0,4},{4,0},{8,12},{12,8},{16,20},{20,16},{24,28},{28,24},{1,5},{5... | collective-permute-start | bytes 1081352 | tf_op jit(solution)/shard_map/ppermute | solution.py:553
  86.7 3.7 %collective-permute-start.13 = (f32[704,128]{1,0:T(8,128)}, f32[704,128]{1,0:T(8,128)}, u32[]{:S(2)}, u32[]{:S(2)}) collective-permute-start(f32[704,128]{1,0:T(8,128)} %collective-permute-done.9.k3), channel_id=1, source_target_pairs={{0,4},{4,0},{8,12},{12,8},{16,20},{20,16},{24,28},{28,24},{1,5},{5... | collective-permute-start | bytes 1081352 | tf_op jit(solution)/shard_map/ppermute | solution.py:553
  90.4 11.9 %copy-start.3 = (f32[512,512]{1,0:T(8,128)S(1)}, f32[512,512]{1,0:T(8,128)}, u32[]{:S(2)}) copy-start(f32[512,512]{1,0:T(8,128)} %rows_ref.3) | copy-start | bytes 3145732

commit v2 on v1

--- a/solution.py
+++ b/solution.py
@@ -10,6 +10,8 @@
 CAP = 96
 PEERS = 16
 SLOTS = PEERS * CAP
+SOME = 64
+FEW = PEERS * SOME
 HALF = (NB + 2 * CAP) // 2
 RD = ("row", "depth")
 F32 = jnp.float32
@@ -77,12 +79,9 @@
 
 
 def running(x):
-    lane = iota(x.shape, 1)
-    by = 1
-    while by < x.shape[1]:
-        x = x + jnp.where(lane >= by, pltpu.roll(x, by, 1), 0.0)
-        by *= 2
-    return x
+    n = x.shape[1]
+    upto = jnp.where(iota((n, n), 0) <= iota((n, n), 1), 1.0, 0.0).astype(BF16)
+    return mm(x.astype(BF16), upto)
 
 
 def down(mask, value):
@@ -115,17 +114,28 @@
         jnp.where(taken, -1.0, two),
     )
     owner = source.astype(jnp.int32) >> 9
-    owners = jnp.where(iota((PEERS, 2 * NB), 0) == owner, 1.0, 0.0)
-    count = running(owners)
-    rank = jnp.sum(owners * count, axis=0, keepdims=True) - 1.0
+    peer = iota((PEERS, NB), 0)
     takers = [v.astype(jnp.int32) >> 9 for v in leaves]
-    taker_rows = jnp.concatenate([jnp.where(iota((PEERS, NB), 0) == t, 1.0, 0.0) for t in takers], axis=0)
-    taker_count = taker_rows * running(taker_rows)
+    parties = [owner[:, :NB], owner[:, NB:], *takers]
+    shown = jnp.concatenate([jnp.where(peer == p, 1.0, 0.0) for p in parties], axis=0)
+    count = running(shown)
+    ranks = shown * (count - 1.0)
+    rank_one, rank_two, *taker_rank = [
+        jnp.sum(ranks[n * PEERS:(n + 1) * PEERS], axis=0, keepdims=True) for n in range(4)
+    ]
+    number_one, number_two, *number = [count[n * PEERS:(n + 1) * PEERS, NB - 1:] for n in range(4)]
+    in_one = jnp.minimum(number_one, float(SOME))
+    longest = [jnp.max(v, axis=0, keepdims=True) for v in number]
+    peer = iota((PEERS, 1), 0)
+    start_two = in_one + jnp.where(peer == 0, longest[0], jnp.where(peer == 1, longest[1], 0.0))
+    start_two = jnp.maximum(start_two, jnp.maximum(CAP - number_two, float(CAP - SOME)))
+    place_two = rank_two + jnp.sum(shown[PEERS:2 * PEERS] * start_two, axis=0, keepdims=True)
+    place_one = jnp.where(rank_one < SOME, rank_one, rank_one + 2048.0)
+    rank = jnp.concatenate([place_one, place_two], axis=1)
     most = jnp.max(rank)
     out_codes, in_codes = [], []
     for q in range(2):
-        sent = count[q:q + 1, 2 * NB - 1:]
-        place = jnp.sum(taker_count[q * PEERS:(q + 1) * PEERS], axis=0, keepdims=True) - 1.0 + sent
+        place = taker_rank[q] + in_one[q:q + 1]
         place = place.astype(jnp.int32)
         most = jnp.maximum(most, jnp.max(jnp.where(takers[q] < 0, 0, place).astype(F32)))
         out_codes.append(jnp.where(takers[q] >= 0, takers[q] * 4096 + place, -1))
@@ -188,8 +198,15 @@
 
 
 def slots_of(at_ref, n):
-    at = column(in_first(at_ref[:, n * NB:(n + 1) * NB]))
-    return jnp.where(iota((NB, SLOTS), 1) == at, 1.0, 0.0).astype(BF16)
+    code = at_ref[:, n * NB:(n + 1) * NB]
+    place = code & 4095
+    at = column(jnp.where(place < CAP, (code >> 12) * SOME + place - n * (CAP - SOME), -1))
+    return jnp.where(iota((NB, FEW), 1) == at, 1.0, 0.0).astype(BF16)
+
+
+def share(got, n):
+    some = got[:, :SOME] if n == 0 else got[:, CAP - SOME:]
+    return some.reshape(FEW, got.shape[2])
 
 
 def arrivals(at_ref):
@@ -198,31 +215,33 @@
     return jnp.where(iota((NB, 2 * CAP), 1) == at, 1.0, 0.0).astype(BF16), column(code) >= 0
 
 
-def late(flag_ref, extra_ref, buffer, sem):
-    @pl.when(flag_ref[0] < CAP)
-    def _():
-        buffer[...] = jnp.zeros_like(buffer)
-
+def late(flag_ref, extra_ref, buffer, sem, target):
     @pl.when(flag_ref[0] >= CAP)
     def _():
         copy = pltpu.make_async_copy(extra_ref, buffer, sem)
         copy.start()
         copy.wait()
 
-    return buffer
-
-
-def panel_rows_kernel(where_ref, flag_ref, at_ref, got_ref, extra_ref, keep_ref, send_ref, tops_ref, more, sem):
+        def turn(n, carry):
+            at = pl.ds(pl.multiple_of(n * 16, 16), 16)
+            target[at] += buffer[at]
+            return carry
+
+        lax.fori_loop(0, target.shape[0] // 16, turn, 0)
+
+
+def panel_rows_kernel(where_ref, flag_ref, at_ref, got_ref, extra_ref, keep_ref, send_ref, tops_ref, rows, more, sem):
     core = where_ref[1]
-    more = late(flag_ref, extra_ref.at[:2 * NB, :128], more, sem)
-    parts = split2(got_ref[...])
-    first = pick(slots_of(at_ref, 0), parts) + more[:NB]
-    second = pick(slots_of(at_ref, 1), parts) + more[NB:]
+    got = got_ref[...]
+    for n in range(2):
+        rows[n * NB:(n + 1) * NB] = pick(slots_of(at_ref, n), split2(share(got, n)))
+    late(flag_ref, extra_ref.at[:2 * NB, :128], more, sem, rows)
+    first, second = rows[:NB], rows[NB:]
     left = iota((NB, 128), 1) < 64
     tops_ref[...] = jnp.where(left, first, second)
     swapped = jnp.where(left, second, first)
     upper = swapped[:HALF]
-    lower = jnp.concatenate([swapped[HALF:], got_ref[:2 * CAP]], axis=0)
+    lower = jnp.concatenate([swapped[HALF:], got[:2].reshape(2 * CAP, 128)], axis=0)
     keep_ref[...] = jnp.where(core == 0, upper, lower)
     send_ref[...] = jnp.where(core == 0, lower, upper)
 
@@ -234,7 +253,7 @@
         in_specs=[SMEM] * 2 + [VMEM] * 2 + [ANY],
         out_specs=[VMEM] * 3,
         out_shape=[half, half, jax.ShapeDtypeStruct((NB, 128), F32)],
-        scratch_shapes=[pltpu.VMEM((2 * NB, 128), F32), pltpu.SemaphoreType.DMA],
+        scratch_shapes=[pltpu.VMEM((2 * NB, 128), F32), pltpu.VMEM((2 * NB, 128), F32), pltpu.SemaphoreType.DMA],
         name="panel_rows",
     )(where, flag, at, got, extra)
 
@@ -248,7 +267,7 @@
 
 
 def fold(at, lower_inv):
-    shape = jax.ShapeDtypeStruct((2, NB, SLOTS), BF16)
+    shape = jax.ShapeDtypeStruct((2, NB, FEW), BF16)
     return pl.pallas_call(
         fold_kernel, in_specs=[VMEM] * 2, out_specs=[VMEM] * 2, out_shape=[shape, shape], name="fold_slots"
     )(at, lower_inv)
@@ -283,7 +302,6 @@
         zz = lax.rem(z + 4 - s, 4)
         gath[core, zz] = a[...]
         gath[1 - core, zz] = b[...]
-    more = late(flag_ref, extra_ref, more, sem)
     left = iota((2 * HALF, 128), 1) < 64
     ones, twos = [], []
     for zz in range(4):
@@ -294,10 +312,11 @@
     in_one, in_two = jnp.concatenate(ones, axis=1), jnp.concatenate(twos, axis=1)
     onehot, moved = arrivals(at_ref)
     top_two_one, top_one_two = in_one[:NB], in_two[:NB]
-    own_one = jnp.where(moved, pick(onehot, split2(in_one[NB:])) + more[0], whole_ref[0])
-    own_two = jnp.where(moved, pick(onehot, split2(in_two[NB:])) + more[1], whole_ref[1])
-    own_one = jnp.where(me == 1, top_two_one, own_one)
-    own_two = jnp.where(me == 1, 0.0, own_two)
+    src[:NB] = jnp.where(moved, pick(onehot, split2(in_one[NB:])), whole_ref[0])
+    src[NB:] = jnp.where(moved, pick(onehot, split2(in_two[NB:])), whole_ref[1])
+    late(flag_ref, extra_ref, more, sem, src)
+    own_one = jnp.where(me == 1, top_two_one, src[:NB])
+    own_two = jnp.where(me == 1, 0.0, src[NB:])
     upper_one_inv = split2(upper_ref[0])
     lower_kept = dot3_upper(split2(own_one), upper_one_inv)
     lower_top = dot3_upper(split2(top_two_one), upper_one_inv)
@@ -308,11 +327,11 @@
     left_ref[0], left_ref[1] = kept_parts
     left_ref[2], left_ref[3] = split2(lower_two)
     left_ref[4], left_ref[5] = split2(dot3_lower(split2(lower_ref[1]), split2(lower_top)))
-    src[0] = lower_kept
-    src[1] = jnp.where(me == 0, upper_panel, jnp.where(me == 1, updated, lower_two))
+    src[:NB] = lower_kept
+    src[NB:] = jnp.where(me == 0, upper_panel, jnp.where(me == 1, updated, lower_two))
     at = pl.multiple_of(z * 128, 128)
-    one = src[0, :, pl.ds(at, 128)]
-    two = src[1, :, pl.ds(at, 128)]
+    one = src[:NB, pl.ds(at, 128)]
+    two = src[NB:, pl.ds(at, 128)]
     left = iota((NB, 128), 1) < 64
     mine = jnp.where(
         core == 0,
@@ -333,8 +352,8 @@
         out_shape=[jax.ShapeDtypeStruct((6, NB, NB), BF16), jax.ShapeDtypeStruct((128, NB), F32)],
         scratch_shapes=[
             pltpu.VMEM((2, 4, 2 * HALF, 128), F32),
-            pltpu.VMEM((2, NB, NB), F32),
-            pltpu.VMEM((2, NB, NB), F32),
+            pltpu.VMEM((2 * NB, NB), F32),
+            pltpu.VMEM((2 * NB, NB), F32),
             pltpu.SemaphoreType.DMA,
         ],
         name="panel_math",
@@ -345,29 +364,21 @@
 
 
 def slab_kernel(where_ref, flag_ref, at_ref, got_ref, rows_ref, extra_ref, one_ref, two_ref, left_ref, out_ref,
-                more, sem):
+                parts, more, sem):
     me = where_ref[0]
     at = pl.multiple_of(pl.program_id(0) * WIDE, WIDE)
-    more = late(flag_ref, extra_ref.at[:, pl.ds(at, WIDE)], more, sem)
-    got = split2(got_ref[...])
-    upper_one = dot3((one_ref[0], one_ref[1]), got) + more[:NB]
+    got = got_ref[...]
+    onehot, moved = arrivals(at_ref)
+    parts[2 * NB:] = jnp.where(moved, pick(onehot, split2(got[:2].reshape(2 * CAP, WIDE))), rows_ref[...])
+    parts[:NB] = dot3((one_ref[0], one_ref[1]), split2(share(got, 0)))
+    parts[NB:2 * NB] = dot3((two_ref[0], two_ref[1]), split2(share(got, 1)))
+
+    late(flag_ref, extra_ref.at[:, pl.ds(at, WIDE)], more, sem, parts)
+    upper_one = parts[:NB]
     one = split2(upper_one)
-    upper_two = (dot3((two_ref[0], two_ref[1]), got) - dot3((left_ref[4], left_ref[5]), one)) + more[NB:2 * NB]
-
-    @pl.when(me == 0)
-    def _():
-        out_ref[...] = upper_one
-
-    @pl.when(me == 1)
-    def _():
-        out_ref[...] = upper_two
-
-    @pl.when(me > 1)
-    def _():
-        onehot, moved = arrivals(at_ref)
-        own = jnp.where(moved, pick(onehot, split2(got_ref[:2 * CAP])) + more[2 * NB:], rows_ref[...])
-        two = split2(upper_two)
-        out_ref[...] = own - dot3((left_ref[0], left_ref[1]), one) - dot3((left_ref[2], left_ref[3]), two)
+    upper_two = parts[NB:2 * NB] - dot3((left_ref[4], left_ref[5]), one)
+    schur = parts[2 * NB:] - dot3((left_ref[0], left_ref[1]), one) - dot3((left_ref[2], left_ref[3]), split2(upper_two))
+    out_ref[...] = jnp.where(me == 0, upper_one, jnp.where(me == 1, upper_two, schur))
 
 
 def slab_math(where, flag, at, got, rows, extra, one, two, left):
@@ -379,16 +390,16 @@
             SMEM,
             SMEM,
             whole(1, 3 * NB),
-            pl.BlockSpec((SLOTS, WIDE), lambda i: (0, i)),
+            pl.BlockSpec((PEERS, CAP, WIDE), lambda i: (0, 0, i)),
             pl.BlockSpec((NB, WIDE), lambda i: (0, i)),
             ANY,
-            whole(2, NB, SLOTS),
-            whole(2, NB, SLOTS),
+            whole(2, NB, FEW),
+            whole(2, NB, FEW),
             whole(6, NB, NB),
         ],
         out_specs=pl.BlockSpec((NB, WIDE), lambda i: (0, i)),
         out_shape=jax.ShapeDtypeStruct((NB, NB), F32),
-        scratch_shapes=[pltpu.VMEM((3 * NB, WIDE), F32), pltpu.SemaphoreType.DMA],
+        scratch_shapes=[pltpu.VMEM((3 * NB, WIDE), F32), pltpu.VMEM((3 * NB, WIDE), F32), pltpu.SemaphoreType.DMA],
         name="slab_math",
     )(where, flag, at, got, rows, extra, one, two, left)
 
@@ -405,7 +416,7 @@
 
 def exchange(blocks):
     width = blocks.shape[1]
-    return lax.all_to_all(blocks.reshape(PEERS, CAP, width), RD, 0, 0).reshape(SLOTS, width)
+    return lax.all_to_all(blocks.reshape(PEERS, CAP, width), RD, 0, 0)
 
 
 def unused_kernel(*refs):
@@ -498,8 +509,8 @@
 def late_panel_kernel(in_ref, out_ref):
     left = iota((NB, 128), 1) < 64
     a, b = in_ref[0], in_ref[1]
-    out_ref[0] = jnp.where(left, a, pltpu.roll(b, 64, 1))
-    out_ref[1] = jnp.where(left, pltpu.roll(a, 64, 1), b)
+    out_ref[:NB] = jnp.where(left, a, pltpu.roll(b, 64, 1))
+    out_ref[NB:] = jnp.where(left, pltpu.roll(a, 64, 1), b)
 
 
 def late_panel(pieces):
@@ -507,8 +518,8 @@
         late_panel_kernel,
         grid=(4,),
         in_specs=[pl.BlockSpec((2, NB, 128), lambda i: (i, 0, 0))],
-        out_specs=pl.BlockSpec((2, NB, 128), lambda i: (0, 0, i)),
-        out_shape=jax.ShapeDtypeStruct((2, NB, NB), F32),
+        out_specs=pl.BlockSpec((2 * NB, 128), lambda i: (0, i)),
+        out_shape=jax.ShapeDtypeStruct((2 * NB, NB), F32),
         name="late_panel",
     )(pieces)
 
@@ -545,7 +556,7 @@
         wide = late_panel(late_gather(rows[2 * NB:, :128], col))
         return r + 1, rows, wide, late_product(lower_inv, rows)
 
-    start = (jnp.int32(1), *unwritten((3 * NB, 128 + NB), (2, NB, NB), (3 * NB, NB)))
+    start = (jnp.int32(1), *unwritten((3 * NB, 128 + NB), (2 * NB, NB), (3 * NB, NB)))
     return lax.while_loop(lambda s: s[0] * CAP <= most, turn, start)[1:]
 
 

time: 118 us -> 117 us (level)
  the two profiles are of different devices: /device:TPU:5 before, /device:TPU:1 now
where the time goes in v2:
time: 117 us
  Pallas kernels  49.1 us (42%)
  waiting for transfers between devices  36.1 us (31%)
  starting transfers between devices  25.6 us (22%)
  local copies, waits for them, and re-layouts  2.78 us (2%)
  other arithmetic  1.65 us (1%)
    ppermute x6, waiting for transfers between devices, shift(): lax.ppermute(x, 'col', [(c, (c // 2 + by) % 4 * 2 + c % 2) for c in range...  30 us
    pallas_call x1, Pallas kernels, slab_math(): pl.pallas_call(slab_kernel, grid=(NB // WIDE,), in_specs=[SMEM, SMEM, who...  14 us
    pallas_call x1, Pallas kernels, panel_math(): pl.pallas_call(panel_math_kernel, in_specs=[SMEM] * 2 + [VMEM] * 3 + [ANY...  12.3 us
    all_to_all x2, starting transfers between devices, exchange(): return lax.all_to_all(blocks.reshape(PEERS, CAP, width), RD, 0, 0)  12.2 us
    ppermute x6, starting transfers between devices, shift(): lax.ppermute(x, 'col', [(c, (c // 2 + by) % 4 * 2 + c % 2) for c in range...  8.53 us
    all_to_all x2, waiting for transfers between devices, exchange(): return lax.all_to_all(blocks.reshape(PEERS, CAP, width), RD, 0, 0)  6.08 us
    pallas_call x1, Pallas kernels, pack(): pl.pallas_call(pack_kernel, grid=(4,), in_specs=[pl.BlockSpec((8, NB), la...  4.98 us
    ppermute x6, starting transfers between devices, partner(): return lax.ppermute(x, 'col', [(c, c ^ 1) for c in range(8)])  4.83 us
  transfers between devices with their start and end apart: 14, of which 3 were waited for; matrix products, arithmetic and copies ran while one was open for 2% of the time, Pallas kernels for 26%

profile of v2, /device:TPU:1, one launch (start us, length us, event | category | flops | bytes accessed | tf_op | source)
XLA Modules:
  0.0 116.8 jit_solution(12014443300484256461)
XLA Ops:
  0.7 0.7 pad_add_fusion.where_ref
  1.3 4.4 %make_plan.1 = (s32[8,512]{1,0:T(8,128)S(1)}, s32[1,1536]{1,0:T(1,128)S(1)}, s32[1]{0:T(128)}, f32[1536,128]{1,0:T(8,128)}) custom-call(s32[4]{0:T(128)} %pad_add_fusion.where_ref, s32[1,512]{1,0:T(1,128)} %bitcast.27, s32[1,512]{1,0:T(1,128)} %bitcast.28, f32[128,512]{1,0:T(8,128)} %bitcast.22), custom_call_target="tpu_custom_call" | custom-call | tf_op jit(solution)/shard_map/make_plan/pallas_call | solution.py:161
  5.7 7.6 %all-to-all-start = ((f32[16,96,128]{2,1,0:T(8,128)}), f32[16,96,128]{2,1,0:T(8,128)S(1)}, u32[]{:S(2)}, u32[]{:S(2)}) async-start(f32[16,96,128]{2,1,0:T(8,128)} %bitcast.26), calls=%async_computation | async-start | bytes 1572864 | tf_op jit(solution)/shard_map/all_to_all | solution.py:419
  13.3 1.0 collective-permute-start.2
  14.4 1.1 mark.1.flag_ref
  15.5 5.0 %pack_rows.1 = f32[1536,512]{1,0:T(8,128)} custom-call(s32[8,512]{1,0:T(8,128)S(1)} %get-tuple-element.808.codes_ref, f32[512,512]{1,0:T(8,128)} %rows_ref.3), custom_call_target="tpu_custom_call" | custom-call | tf_op jit(solution)/shard_map/pack_rows/pallas_call | solution.py:189
  20.5 6.1 %all-to-all-done.got_ref = f32[16,96,128]{2,1,0:T(8,128)S(1)} async-done(((f32[16,96,128]{2,1,0:T(8,128)}), f32[16,96,128]{2,1,0:T(8,128)S(1)}, u32[]{:S(2)}, u32[]{:S(2)}) %all-to-all-start) | async-done | bytes 786464 | tf_op jit(solution)/shard_map/all_to_all | solution.py:419
  26.6 0.9 copy-done.5
  27.5 4.6 %all-to-all-start.1 = ((f32[16,96,512]{2,1,0:T(8,128)}), f32[16,96,512]{2,1,0:T(8,128)}, u32[]{:S(2)}, u32[]{:S(2)}) async-start(f32[16,96,512]{2,1,0:T(8,128)} %bitcast.25), calls=%async_computation.1 | async-start | bytes 6291456 | tf_op jit(solution)/shard_map/all_to_all | solution.py:419
  32.1 0.0 copy-done.1
  32.1 0.0 copy-done.4
  32.1 0.7 while.66
  32.8 0.0 copy-start
  32.8 3.9 %panel_rows.1 = (f32[352,128]{1,0:T(8,128)}, f32[352,128]{1,0:T(8,128)}, f32[512,128]{1,0:T(8,128)}) custom-call(s32[4]{0:T(128)} %pad_add_fusion.where_ref, s32[1]{0:T(128)} %mark.1.flag_ref, s32[1,1536]{1,0:T(1,128)S(1)} %get-tuple-element.897, f32[16,96,128]{2,1,0:T(8,128)} %copy-done.5, f32[1536,640]{1,0:T(8,128)} %get-tuple-element.888), custom_call_target="tpu_custom_call" | custom-call | tf_op jit(solution)/shard_map/panel_rows/pallas_call | solution.py:251
  36.7 2.3 %collective-permute-start.6 = (f32[352,128]{1,0:T(8,128)}, f32[352,128]{1,0:T(8,128)S(1)}, u32[]{:S(2)}, u32[]{:S(2)}) collective-permute-start(f32[352,128]{1,0:T(8,128)} %get-tuple-element.536), channel_id=1, source_target_pairs={{0,4},{4,0},{8,12},{12,8},{16,20},{20,16},{24,28},{28,24},{1,5},{5... | collective-permute-start | bytes 540680 | tf_op jit(solution)/shard_map/ppermute | solution.py:564
  39.0 0.0 collective-permute-done.2
  39.0 1.0 pad_maximum_fusion.p0
  40.0 0.0 copy-start.6
  40.0 1.1 constant_dynamic-update-slice_fusion.1
  41.1 0.0 collective-permute-done.6
  41.2 0.0 copy-start.7
  41.2 1.7 %collective-permute-start.7 = (f32[704,128]{1,0:T(8,128)S(1)}, f32[704,128]{1,0:T(8,128)S(1)}, u32[]{:S(2)}, u32[]{:S(2)}) collective-permute-start(f32[704,128]{1,0:T(8,128)S(1)} %constant_dynamic-update-slice_fusion.k0), channel_id=1, source_target_pairs={{0,8},{4,12},{8,16},{12,20},{16,24},{20,28},{24,0},{28,4},{1,9},{5... | collective-permute-start | bytes 1081352 | tf_op jit(solution)/shard_map/ppermute | solution.py:568
  42.9 1.6 %collective-permute-start.3 = (f32[256,512]{1,0:T(8,128)S(1)}, f32[256,512]{1,0:T(8,128)}, u32[]{:S(2)}, u32[]{:S(2)}) collective-permute-start(f32[256,512]{1,0:T(8,128)S(1)} %pad_maximum_fusion.p0), channel_id=1, source_target_pairs={{0,8},{4,12},{8,16},{12,20},{16,24},{20,28},{24,0},{28,4},{1,9},{5... | collective-permute-start | bytes 1572872 | tf_op jit(solution)/shard_map/ppermute | solution.py:568
  44.5 1.7 %collective-permute-start.4 = (f32[256,512]{1,0:T(8,128)S(1)}, f32[256,512]{1,0:T(8,128)}, u32[]{:S(2)}, u32[]{:S(2)}) collective-permute-start(f32[256,512]{1,0:T(8,128)S(1)} %pad_maximum_fusion.p0), channel_id=1, source_target_pairs={{0,16},{4,20},{8,24},{12,28},{16,0},{20,4},{24,8},{28,12},{1,17},{... | collective-permute-start | bytes 1572872 | tf_op jit(solution)/shard_map/ppermute | solution.py:568
  46.3 1.2 %collective-permute-start.8 = (f32[704,128]{1,0:T(8,128)S(1)}, f32[704,128]{1,0:T(8,128)}, u32[]{:S(2)}, u32[]{:S(2)}) collective-permute-start(f32[704,128]{1,0:T(8,128)S(1)} %constant_dynamic-update-slice_fusion.k0), channel_id=1, source_target_pairs={{0,16},{4,20},{8,24},{12,28},{16,0},{20,4},{24,8},{28,12},{1,17},{... | collective-permute-start | bytes 1081352 | tf_op jit(solution)/shard_map/ppermute | solution.py:568
  47.5 1.0 collective-permute-start.9
  48.5 5.3 %collective-permute-done.7.k1 = f32[704,128]{1,0:T(8,128)S(1)} collective-permute-done((f32[704,128]{1,0:T(8,128)S(1)}, f32[704,128]{1,0:T(8,128)S(1)}, u32[]{:S(2)}, u32[]{:S(2)}) %collective-permute-start.7) | collective-permute-done | bytes 360480 | tf_op jit(solution)/shard_map/ppermute | solution.py:568
  53.9 0.7 copy-done.8
  54.6 1.2 %collective-permute-start.5 = (f32[256,512]{1,0:T(8,128)S(1)}, f32[256,512]{1,0:T(8,128)}, u32[]{:S(2)}, u32[]{:S(2)}) collective-permute-start(f32[256,512]{1,0:T(8,128)S(1)} %pad_maximum_fusion.p0), channel_id=1, source_target_pairs={{0,24},{4,28},{8,0},{12,4},{16,8},{20,12},{24,16},{28,20},{1,25},{... | collective-permute-start | bytes 1572872 | tf_op jit(solution)/shard_map/ppermute | solution.py:568
  55.8 4.5 %fold_slots.1 = (bf16[2,512,1024]{2,1,0:T(8,128)(2,1)}, bf16[2,512,1024]{2,1,0:T(8,128)(2,1)}) custom-call(s32[1,1536]{1,0:T(1,128)S(1)} %get-tuple-element.897, f32[2,512,512]{2,1,0:T(8,128)S(1)} %copy-done), custom_call_target="tpu_custom_call" | custom-call | tf_op jit(solution)/shard_map/fold_slots/pallas_call | solution.py:271
  60.4 24.6 %collective-permute-done.8.k2 = f32[704,128]{1,0:T(8,128)} collective-permute-done((f32[704,128]{1,0:T(8,128)S(1)}, f32[704,128]{1,0:T(8,128)}, u32[]{:S(2)}, u32[]{:S(2)}) %collective-permute-start.8) | collective-permute-done | bytes 360480 | tf_op jit(solution)/shard_map/ppermute | solution.py:568
  85.0 0.9 collective-permute-start.10
  85.9 0.0 collective-permute-done.9.k3
  85.9 0.0 collective-permute-start.11
  85.9 0.0 collective-permute-done.3.p1
  85.9 0.5 collective-permute-start.12
  86.4 0.0 collective-permute-done.4.p2
  86.4 0.1 collective-permute-start.13
  86.5 0.0 collective-permute-done.5.p3
  86.5 3.7 %own_panels.1.whole_ref = f32[2,512,512]{2,1,0:T(8,128)} custom-call(s32[4]{0:T(128)} %pad_add_fusion.where_ref, f32[256,512]{1,0:T(8,128)} %copy-done.6, f32[256,512]{1,0:T(8,128)} %collective-permute-done.3.p1, f32[256,512]{1,0:T(8,128)} %collective-permute-done.4.p2, f32[256,512]{1,0:T(8,128)} %collective-permute-done.5.p3), custom_call_target="tpu_custom_call" | custom-call | tf_op jit(solution)/shard_map/own_panels/pallas_call | solution.py:288
  90.2 0.0 collective-permute-done.10.p0
  90.2 0.0 collective-permute-done.11.p1
  90.2 0.0 collective-permute-done.12.p2
  90.2 0.0 collective-permute-done.13.p3
  90.2 0.0 copy-start.3
  90.2 12.3 %panel_math.1 = (bf16[6,512,512]{2,1,0:T(8,128)(2,1)}, f32[128,512]{1,0:T(8,128)}) custom-call(s32[4]{0:T(128)} %pad_add_fusion.where_ref, s32[1]{0:T(128)} %mark.1.flag_ref, s32[1,1536]{1,0:T(1,128)S(1)} %get-tuple-element.897, f32[512,128]{1,0:T(8,128)} %get-tuple-element.533.tops_ref, f32[2,512,512]{2,1,0:T(8,128)} %own_panels.1.whole_ref, ...), custom_call_target="tpu_custom_call" | custom-call | tf_op jit(solution)/shard_map/panel_math/pallas_call | solution.py:348
  102.6 0.0 all-to-all-done.1.got_ref
  102.6 14.0 %slab_math.1 = f32[512,512]{1,0:T(8,128)} custom-call(s32[4]{0:T(128)} %pad_add_fusion.where_ref, s32[1]{0:T(128)} %mark.1.flag_ref, s32[1,1536]{1,0:T(1,128)S(1)} %get-tuple-element.897, f32[16,96,512]{2,1,0:T(8,128)} %all-to-all-done.1.got_ref, f32[512,512]{1,0:T(8,128)S(1)} %copy-done.3, f32[1536,512]{1,0:T(8,128)} %get-tuple-element.890, ...), custom_call_target="tpu_custom_call" | custom-call | tf_op jit(solution)/shard_map/slab_math/pallas_call | solution.py:386
  (10 shorter events, 0.0 us)
Async XLA Ops:
  5.7 20.8 %all-to-all-start = ((f32[16,96,128]{2,1,0:T(8,128)}), f32[16,96,128]{2,1,0:T(8,128)S(1)}, u32[]{:S(2)}, u32[]{:S(2)}) async-start(f32[16,96,128]{2,1,0:T(8,128)} %bitcast.26), calls=%async_computation | async-start | bytes 1572864 | tf_op jit(solution)/shard_map/all_to_all | solution.py:419
  13.3 25.7 %collective-permute-start.2 = (f32[128,512]{1,0:T(8,128)}, f32[128,512]{1,0:T(8,128)}, u32[]{:S(2)}, u32[]{:S(2)}) collective-permute-start(f32[128,512]{1,0:T(8,128)} %bitcast.23), channel_id=1, source_target_pairs={{0,4},{4,0},{8,12},{12,8},{16,20},{20,16},{24,28},{28,24},{1,5},{5... | collective-permute-start | bytes 786440 | tf_op jit(solution)/shard_map/ppermute | solution.py:564
  26.6 0.9 copy-start.5
  27.5 4.6 %copy-start.1 = (f32[512,512]{1,0:T(8,128)S(1)}, f32[512,512]{1,0:T(8,128)}, u32[]{:S(2)}) copy-start(f32[512,512]{1,0:T(8,128)} %rows_ref.3) | copy-start | bytes 3145732
  27.5 4.6 %copy-start.4 = (f32[2,512,64]{1,2,0:T(8,128)S(1)}, f32[2,512,64]{1,2,0:T(8,128)}, u32[]{:S(2)}) copy-start(f32[2,512,64]{1,2,0:T(8,128)} %param.12) | copy-start | bytes 786436
  27.5 75.1 %all-to-all-start.1 = ((f32[16,96,512]{2,1,0:T(8,128)}), f32[16,96,512]{2,1,0:T(8,128)}, u32[]{:S(2)}, u32[]{:S(2)}) async-start(f32[16,96,512]{2,1,0:T(8,128)} %bitcast.25), calls=%async_computation.1 | async-start | bytes 6291456 | tf_op jit(solution)/shard_map/all_to_all | solution.py:419
  32.8 23.0 %copy-start = (f32[2,512,512]{2,1,0:T(8,128)S(1)}, f32[2,512,512]{2,1,0:T(8,128)}, u32[]{:S(2)}) copy-start(f32[2,512,512]{2,1,0:T(8,128)} %get-tuple-element.899) | copy-start | bytes 6291460
  36.7 4.5 %collective-permute-start.6 = (f32[352,128]{1,0:T(8,128)}, f32[352,128]{1,0:T(8,128)S(1)}, u32[]{:S(2)}, u32[]{:S(2)}) collective-permute-start(f32[352,128]{1,0:T(8,128)} %get-tuple-element.536), channel_id=1, source_target_pairs={{0,4},{4,0},{8,12},{12,8},{16,20},{20,16},{24,28},{28,24},{1,5},{5... | collective-permute-start | bytes 540680 | tf_op jit(solution)/shard_map/ppermute | solution.py:564
  40.0 46.5 %copy-start.6 = (f32[256,512]{1,0:T(8,128)}, f32[256,512]{1,0:T(8,128)S(1)}, u32[]{:S(2)}) copy-start(f32[256,512]{1,0:T(8,128)S(1)} %pad_maximum_fusion.p0) | copy-start | bytes 1572868
  41.2 49.0 %copy-start.7 = (f32[704,128]{1,0:T(8,128)}, f32[704,128]{1,0:T(8,128)S(1)}, u32[]{:S(2)}) copy-start(f32[704,128]{1,0:T(8,128)S(1)} %constant_dynamic-update-slice_fusion.k0) | copy-start | bytes 1081348
  41.2 12.7 %collective-permute-start.7 = (f32[704,128]{1,0:T(8,128)S(1)}, f32[704,128]{1,0:T(8,128)S(1)}, u32[]{:S(2)}, u32[]{:S(2)}) collective-permute-start(f32[704,128]{1,0:T(8,128)S(1)} %constant_dynamic-update-slice_fusion.k0), channel_id=1, source_target_pairs={{0,8},{4,12},{8,16},{12,20},{16,24},{20,28},{24,0},{28,4},{1,9},{5... | collective-permute-start | bytes 1081352 | tf_op jit(solution)/shard_map/ppermute | solution.py:568
  42.9 43.0 %collective-permute-start.3 = (f32[256,512]{1,0:T(8,128)S(1)}, f32[256,512]{1,0:T(8,128)}, u32[]{:S(2)}, u32[]{:S(2)}) collective-permute-start(f32[256,512]{1,0:T(8,128)S(1)} %pad_maximum_fusion.p0), channel_id=1, source_target_pairs={{0,8},{4,12},{8,16},{12,20},{16,24},{20,28},{24,0},{28,4},{1,9},{5... | collective-permute-start | bytes 1572872 | tf_op jit(solution)/shard_map/ppermute | solution.py:568
  44.5 41.8 %collective-permute-start.4 = (f32[256,512]{1,0:T(8,128)S(1)}, f32[256,512]{1,0:T(8,128)}, u32[]{:S(2)}, u32[]{:S(2)}) collective-permute-start(f32[256,512]{1,0:T(8,128)S(1)} %pad_maximum_fusion.p0), channel_id=1, source_target_pairs={{0,16},{4,20},{8,24},{12,28},{16,0},{20,4},{24,8},{28,12},{1,17},{... | collective-permute-start | bytes 1572872 | tf_op jit(solution)/shard_map/ppermute | solution.py:568
  46.3 38.7 %collective-permute-start.8 = (f32[704,128]{1,0:T(8,128)S(1)}, f32[704,128]{1,0:T(8,128)}, u32[]{:S(2)}, u32[]{:S(2)}) collective-permute-start(f32[704,128]{1,0:T(8,128)S(1)} %constant_dynamic-update-slice_fusion.k0), channel_id=1, source_target_pairs={{0,16},{4,20},{8,24},{12,28},{16,0},{20,4},{24,8},{28,12},{1,17},{... | collective-permute-start | bytes 1081352 | tf_op jit(solution)/shard_map/ppermute | solution.py:568
  47.5 38.4 %collective-permute-start.9 = (f32[704,128]{1,0:T(8,128)S(1)}, f32[704,128]{1,0:T(8,128)}, u32[]{:S(2)}, u32[]{:S(2)}) collective-permute-start(f32[704,128]{1,0:T(8,128)S(1)} %constant_dynamic-update-slice_fusion.k0), channel_id=1, source_target_pairs={{0,24},{4,28},{8,0},{12,4},{16,8},{20,12},{24,16},{28,20},{1,25},{... | collective-permute-start | bytes 1081352 | tf_op jit(solution)/shard_map/ppermute | solution.py:568
  53.9 0.7 copy-start.8
  54.6 31.9 %collective-permute-start.5 = (f32[256,512]{1,0:T(8,128)S(1)}, f32[256,512]{1,0:T(8,128)}, u32[]{:S(2)}, u32[]{:S(2)}) collective-permute-start(f32[256,512]{1,0:T(8,128)S(1)} %pad_maximum_fusion.p0), channel_id=1, source_target_pairs={{0,24},{4,28},{8,0},{12,4},{16,8},{20,12},{24,16},{28,20},{1,25},{... | collective-permute-start | bytes 1572872 | tf_op jit(solution)/shard_map/ppermute | solution.py:568
  85.0 5.2 %collective-permute-start.10 = (f32[704,128]{1,0:T(8,128)S(1)}, f32[704,128]{1,0:T(8,128)}, u32[]{:S(2)}, u32[]{:S(2)}) collective-permute-start(f32[704,128]{1,0:T(8,128)S(1)} %constant_dynamic-update-slice_fusion.k0), channel_id=1, source_target_pairs={{0,4},{4,0},{8,12},{12,8},{16,20},{20,16},{24,28},{28,24},{1,5},{5... | collective-permute-start | bytes 1081352 | tf_op jit(solution)/shard_map/ppermute | solution.py:564
  85.9 4.3 %collective-permute-start.11 = (f32[704,128]{1,0:T(8,128)}, f32[704,128]{1,0:T(8,128)}, u32[]{:S(2)}, u32[]{:S(2)}) collective-permute-start(f32[704,128]{1,0:T(8,128)} %copy-done.8), channel_id=1, source_target_pairs={{0,4},{4,0},{8,12},{12,8},{16,20},{20,16},{24,28},{28,24},{1,5},{5... | collective-permute-start | bytes 1081352 | tf_op jit(solution)/shard_map/ppermute | solution.py:564
  85.9 4.3 %collective-permute-start.12 = (f32[704,128]{1,0:T(8,128)}, f32[704,128]{1,0:T(8,128)}, u32[]{:S(2)}, u32[]{:S(2)}) collective-permute-start(f32[704,128]{1,0:T(8,128)} %collective-permute-done.8.k2), channel_id=1, source_target_pairs={{0,4},{4,0},{8,12},{12,8},{16,20},{20,16},{24,28},{28,24},{1,5},{5... | collective-permute-start | bytes 1081352 | tf_op jit(solution)/shard_map/ppermute | solution.py:564
  86.4 3.8 %collective-permute-start.13 = (f32[704,128]{1,0:T(8,128)}, f32[704,128]{1,0:T(8,128)}, u32[]{:S(2)}, u32[]{:S(2)}) collective-permute-start(f32[704,128]{1,0:T(8,128)} %collective-permute-done.9.k3), channel_id=1, source_target_pairs={{0,4},{4,0},{8,12},{12,8},{16,20},{20,16},{24,28},{28,24},{1,5},{5... | collective-permute-start | bytes 1081352 | tf_op jit(solution)/shard_map/ppermute | solution.py:564
  90.2 12.4 %copy-start.3 = (f32[512,512]{1,0:T(8,128)S(1)}, f32[512,512]{1,0:T(8,128)}, u32[]{:S(2)}) copy-start(f32[512,512]{1,0:T(8,128)} %rows_ref.3) | copy-start | bytes 3145732
